TPU v7x, 512 devices: a whole 4x8x8 slice. The times are simulated.
512 devices in a mesh: seq: 64 (over x, y, z_lo), tp: 8 (over z_hi, core).
Axes of the slice: x: 4, y: 8, z: 8 (z_hi: 4, z_lo: 2; z = z_hi * 2 + z_lo), core: 2. Of those that a mesh axis runs over, the one named last changes fastest.
Arguments:
- hidden_in: bfloat16 [16384, 2048], P('seq', 'tp'), may hold values from -6 to 6
- norm_gain: float32 [2048], replicated, may hold values from 0.1 to 1.9
- norm_bias: float32 [2048], replicated, may hold values from -3 to 3
- qkv_weight: bfloat16 [3, 2048, 2048], P(None, 'seq', 'tp'), may hold values from -0.125 to 0.125
- qkv_bias: float32 [3, 2048], P(None, 'tp'), may hold values from -3 to 3
- out_weight: bfloat16 [2048, 2048], P('tp', 'seq'), may hold values from -0.125 to 0.125
- out_bias: float32 [2048], P('tp'), may hold values from -3 to 3
- key_cache: bfloat16 [147456, 2048], P('seq', 'tp')
- value_cache: bfloat16 [147456, 2048], P('seq', 'tp'), may hold values from -6 to 6
- cached_len: int32 [16], replicated, may hold values from 0 to 8192, as said below
Outputs:
- mixed: bfloat16 [16384, 2048], P('seq', 'tp')
- key_cache_new: bfloat16 [147456, 2048], P('seq', 'tp')
- value_cache_new: bfloat16 [147456, 2048], P('seq', 'tp')
Inputs may be any that keep to these rules, and one draw needn't show every extreme that they name: `cached_len`: some request has exactly 8192 cached positions.
All inputs are finite; a program needn't handle non-finite values.
Results may differ from a plain program's by a relative error of at most 0.035.
Values may be sent and summed in bfloat16 or wider, within the bound.
A program may use at most 64 MiB of HBM per device.

v0:
```python
import math

import jax
import jax.numpy as jnp
from jax import lax
from jax.sharding import PartitionSpec as P

HEADS = 16
HEAD_DIM = 128
REQS = 16


def from_partner(value, axis, bit):
    return lax.ppermute(value, axis, [(i, i ^ 1 << bit) for i in range(lax.axis_size(axis))])


def for_sending(value):
    return jax.tree.map(lambda a: a.astype(jnp.bfloat16) if a.dtype == jnp.float32 else a, value)


def join_partials(earlier, later):
    top_a, num_a, den_a = earlier
    top_b, num_b, den_b = later
    joint = jnp.maximum(top_a, top_b)
    scale_a = jnp.exp(top_a - joint)
    scale_b = jnp.exp(top_b - joint)
    return (
        joint,
        num_a * scale_a[..., None] + num_b * scale_b[..., None],
        den_a * scale_a + den_b * scale_b,
    )


def on_device(
    hidden_in,
    norm_gain,
    norm_bias,
    qkv_weight,
    qkv_bias,
    out_weight,
    out_bias,
    key_cache,
    value_cache,
    cached_len,
):
    features_all = lax.all_gather(hidden_in, "tp", axis=1, tiled=True)
    tok_dev = features_all.shape[0]
    values_f = features_all.astype(jnp.float32)
    row_mean = jnp.mean(values_f, axis=-1, keepdims=True)
    row_var = jnp.mean(jnp.square(values_f - row_mean), axis=-1, keepdims=True)
    normed = ((values_f - row_mean) * lax.rsqrt(row_var + 1e-05) * norm_gain + norm_bias).astype(
        jnp.bfloat16
    )
    head_cols = qkv_weight.shape[2]
    heads_dev = head_cols // HEAD_DIM
    summed = jnp.einsum(
        "td,kdc->ktc",
        normed,
        lax.all_gather(qkv_weight, "seq", axis=1, tiled=True),
        preferred_element_type=jnp.float32,
    )
    projected = (summed + qkv_bias[:, None, :]).astype(jnp.bfloat16)
    group = lax.axis_size("seq") // REQS
    group_bits = group.bit_length() - 1
    seq_index = lax.axis_index("seq")
    local = seq_index % group
    request = seq_index // group
    block_rows = projected
    for bit in range(group_bits):
        partner_rows = from_partner(block_rows, "seq", bit)
        low_side = local // (1 << bit) % 2 == 0
        block_rows = jnp.where(
            low_side,
            jnp.concatenate([block_rows, partner_rows], axis=1),
            jnp.concatenate([partner_rows, block_rows], axis=1),
        )
    queries = block_rows[0]
    fresh_rows = block_rows[1:]
    span = queries.shape[0]
    slots = key_cache.shape[0]
    base_pos = local * slots
    key_pos = base_pos + jnp.arange(slots)
    length = lax.dynamic_index_in_dim(cached_len, request, 0, keepdims=False)
    offsets = key_pos - length
    inside = (offsets >= 0) & (offsets < span)
    padding = jnp.zeros((2, slots, head_cols), jnp.bfloat16)
    padded = jnp.concatenate([padding, fresh_rows, padding], axis=1)
    begin = jnp.clip(base_pos - length + slots, 0, span + slots)
    placed = lax.dynamic_slice_in_dim(padded, begin, slots, 1)
    keys_dev = jnp.where(inside[:, None], placed[0], key_cache)
    values_dev = jnp.where(inside[:, None], placed[1], value_cache)
    slopes = jnp.exp2(
        -8.0
        * (lax.axis_index("tp") * heads_dev + jnp.arange(heads_dev) + 1).astype(jnp.float32)
        / HEADS
    )
    query_pos = length + jnp.arange(span)

    def one_head(head):
        first_col = head * HEAD_DIM
        query_one = lax.dynamic_slice_in_dim(queries, first_col, HEAD_DIM, 1)
        key_one = lax.dynamic_slice_in_dim(keys_dev, first_col, HEAD_DIM, 1)
        value_one = lax.dynamic_slice_in_dim(values_dev, first_col, HEAD_DIM, 1)
        slope = lax.dynamic_index_in_dim(slopes, head, 0, keepdims=False)
        distance = (query_pos[:, None] - key_pos[None, :]).astype(jnp.float32)
        valid = distance >= 0.0
        scores = (
            jnp.dot(query_one, key_one.T, preferred_element_type=jnp.float32) / math.sqrt(HEAD_DIM)
            - slope * distance
        )
        top_score = jnp.max(jnp.where(valid, scores, -1e30), axis=1)
        weights = jnp.where(valid, jnp.exp(scores - top_score[:, None]), 0.0)
        totals = jnp.sum(weights, axis=1)
        numer = jnp.dot(weights.astype(jnp.bfloat16), value_one, preferred_element_type=jnp.float32)
        return (top_score, numer, totals)

    head_tops, head_nums, head_dens = lax.map(one_head, jnp.arange(heads_dev))
    row_top = head_tops.T
    row_num = head_nums.transpose(1, 0, 2)
    row_den = head_dens.T
    joined = (row_top, row_num, row_den)
    for bit in range(group_bits):
        partner = from_partner(
            (for_sending(joined[0]), for_sending(joined[1]), for_sending(joined[2])), "seq", bit
        )
        joined = join_partials(joined, partner)
    own_first = local * tok_dev
    own_num = lax.dynamic_slice_in_dim(joined[1], own_first, tok_dev, 0)
    own_den = lax.dynamic_slice_in_dim(joined[2], own_first, tok_dev, 0)
    attended = (own_num / own_den[..., None]).reshape(tok_dev, head_cols).astype(jnp.bfloat16)
    partial_out = jnp.dot(
        attended,
        lax.all_gather(out_weight, "seq", axis=1, tiled=True),
        preferred_element_type=jnp.float32,
    )
    reduced = lax.psum_scatter(
        partial_out.astype(jnp.bfloat16), "tp", scatter_dimension=1, tiled=True
    ).astype(jnp.float32)
    mixed = (reduced + out_bias).astype(jnp.bfloat16)
    return (mixed, keys_dev, values_dev)


def solution(mesh):
    placed = (
        P("seq", "tp"),
        P(),
        P(),
        P(None, "seq", "tp"),
        P(None, "tp"),
        P("tp", "seq"),
        P("tp"),
        P("seq", "tp"),
        P("seq", "tp"),
        P(),
    )
    return jax.shard_map(
        on_device,
        mesh=mesh,
        in_specs=placed,
        out_specs=(P("seq", "tp"), P("seq", "tp"), P("seq", "tp")),
        check_vma=False,
    )
```

profile of v0, /device:TPU:1, one launch (start us, length us, event | category | flops | bytes accessed | tf_op | source)
XLA Modules:
  0.0 718.9 jit_solution(118338571463301744)
XLA Ops:
  8.7 41.9 %all-gather.4.cloned.1.call-done = bf16[256,2048]{1,0:T(8,128)(2,1)} async-done(((bf16[256,256]{1,0:T(8,128)(2,1)}), bf16[256,2048]{1,0:T(8,128)(2,1)}) %all-gather.4.cloned.1.call-update) | async-done | bytes 1048592 | tf_op jit(solution)/shard_map/all_gather | solution.py:46
  53.7 254.6 %all-gather.6.cloned.1.call-done = bf16[3,2048,256]{2,1,0:T(8,128)(2,1)} async-done(((bf16[3,32,256]{2,1,0:T(8,128)(2,1)}), bf16[3,2048,256]{2,1,0:T(8,128)(2,1)}) %all-gather.6.cloned.1.call-update) | async-done | bytes 3145744 | tf_op jit(solution)/shard_map/all_gather | solution.py:59
  308.3 3.3 fusion.28
  311.6 1.9 collective-permute-start
  313.5 7.5 %collective-permute-done = bf16[3,256,256]{2,1,0:T(8,128)(2,1)S(1)} collective-permute-done((bf16[3,256,256]{2,1,0:T(8,128)(2,1)S(1)}, bf16[3,256,256]{2,1,0:T(8,128)(2,1)S(1)}, u32[]{:S(2)}, u32[]{:S(2)}) %collective-permute-start) | collective-permute-done | bytes 393248 | tf_op jit(solution)/shard_map/ppermute | solution.py:14
  321.4 1.9 collective-permute-start.1
  325.4 9.5 %collective-permute-done.1 = bf16[3,512,256]{2,1,0:T(8,128)(2,1)S(1)} collective-permute-done((bf16[3,512,256]{2,1,0:T(8,128)(2,1)S(1)}, bf16[3,512,256]{2,1,0:T(8,128)(2,1)S(1)}, u32[]{:S(2)}, u32[]{:S(2)}) %collective-permute-start.1) | collective-permute-done | bytes 786464 | tf_op jit(solution)/shard_map/ppermute | solution.py:14
  336.4 5.8 fusion.22
  343.6 40.8 %while.15 = (s32[]{:T(128)}, f32[2,1024]{1,0:T(2,128)S(1)}, f32[2,1024,128]{1,2,0:T(8,128)S(1)}, f32[2,1024]{1,0:T(2,128)S(1)}, s32[2]{0:T(128)S(1)}, /*index=5*...) while((s32[]{:T(128)}, f32[2,1024]{1,0:T(2,128)S(1)}, ...), condition=%wide.region_5.6_spmd.clone, body=%wide.region_2.5_spmd.clone.sunk | while | flops 1269302528 | bytes 68120376 | solution.py:117
  348.3 4.4 select_reduce_fusion.2
  352.7 4.6 fusion.68
  357.3 6.6 fusion.67
  368.7 4.4 select_reduce_fusion.2
  373.1 4.6 fusion.68
  377.7 6.6 fusion.67
  386.5 3.4 collective-permute-start.2
  391.8 3.5 collective-permute-done.2
  395.3 1.9 collective-permute-start.4
  397.3 2.8 collective-permute-done.4
  403.1 3.4 collective-permute-start.7
  406.5 5.6 collective-permute-done.7
  412.1 210.4 %all-gather.8.cloned.1.call-done = bf16[256,2048]{0,1:T(8,128)(2,1)} async-done(((bf16[256,32]{0,1:T(8,128)(2,1)}), bf16[256,2048]{0,1:T(8,128)(2,1)}) %all-gather.8.cloned.1.call-update) | async-done | bytes 1048592 | tf_op jit(solution)/shard_map/all_gather | solution.py:133
  622.5 2.7 convolution_convert_fusion
  625.2 85.6 %reduce-scatter.2.cloned.1.call-done = bf16[256,256]{1,0:T(8,128)(2,1)} async-done(((bf16[256,2048]{1,0:T(8,128)(2,1)}), bf16[256,256]{1,0:T(8,128)(2,1)}) %reduce-scatter.2.cloned.1.call-update) | async-done | bytes 131088 | tf_op jit(solution)/shard_map/reduce_scatter | solution.py:136
  (68 shorter events, 21.7 us)
Async XLA Ops:
  7.2 43.4 %all-gather.4.cloned.1.call-start = ((), (), s32[]{:S(2)}) async-start(), calls=%async_computation.1 | async-start | bytes 1179648 | tf_op jit(solution)/shard_map/all_gather | solution.py:46
  7.9 300.4 %all-gather.6.cloned.1.call-start = ((), (), s32[]{:S(2)}) async-start(), calls=%async_computation.2 | async-start | bytes 3194880 | tf_op jit(solution)/shard_map/all_gather | solution.py:59
  8.6 613.9 %all-gather.8.cloned.1.call-start = ((), (), s32[]{:S(2)}) async-start(), calls=%async_computation.3 | async-start | bytes 1064960 | tf_op jit(solution)/shard_map/all_gather | solution.py:133
  53.7 269.8 %copy-start.6 = (s32[16]{0:T(128)S(1)}, s32[16]{0:T(128)}, u32[]{:S(2)}) copy-start(s32[16]{0:T(128)} %param.21) | copy-start | bytes 196
  311.6 9.5 %collective-permute-start = (bf16[3,256,256]{2,1,0:T(8,128)(2,1)S(1)}, bf16[3,256,256]{2,1,0:T(8,128)(2,1)S(1)}, u32[]{:S(2)}, u32[]{:S(2)}) collective-permute-start(bf16[3,256,256]{2,1,0:T(8,128)(2,1)S(1)} %fusion.28), channel_id=1, source_target_pairs={{0,8},{8,0},{16,24},{24,16},{32,40},{40,32},{48,56},{56,48},{64,72... | collective-permute-start | bytes 1179656 | tf_op jit(solution)/shard_map/ppermute | solution.py:14
  321.4 13.5 %collective-permute-start.1 = (bf16[3,512,256]{2,1,0:T(8,128)(2,1)S(1)}, bf16[3,512,256]{2,1,0:T(8,128)(2,1)S(1)}, u32[]{:S(2)}, u32[]{:S(2)}) collective-permute-start(bf16[3,512,256]{2,1,0:T(8,128)(2,1)S(1)} %maximum_select_fusion.1), channel_id=1, source_target_pairs={{0,16},{8,24},{16,0},{24,8},{32,48},{40,56},{48,32},{56,40},{64,80... | collective-permute-start | bytes 2359304 | tf_op jit(solution)/shard_map/ppermute | solution.py:14
  323.3 387.5 %reduce-scatter.2.cloned.1.call-start = ((), (), s32[]{:S(2)}) async-start(), calls=%async_computation.4 | async-start | bytes 1179648 | tf_op jit(solution)/shard_map/reduce_scatter | solution.py:136
  336.3 5.8 copy-start.1
  336.4 5.8 copy-start.2
  352.7 4.6 copy-start
  373.1 4.6 copy-start
  384.4 15.7 %copy-start.4 = (bf16[2304,256]{1,0:T(8,128)(2,1)}, bf16[2304,256]{1,0:T(8,128)(2,1)S(1)}, u32[]{:S(2)}) copy-start(bf16[2304,256]{1,0:T(8,128)(2,1)S(1)} %get-tuple-element.261) | copy-start | bytes 3538948
  384.5 240.8 %copy-start.3 = (bf16[2304,256]{1,0:T(8,128)(2,1)}, bf16[2304,256]{1,0:T(8,128)(2,1)S(1)}, u32[]{:S(2)}) copy-start(bf16[2304,256]{1,0:T(8,128)(2,1)S(1)} %get-tuple-element.260) | copy-start | bytes 3538948
  384.6 15.6 %collective-permute-start.3 = (bf16[1024,2,128]{0,2,1:T(8,128)(2,1)S(1)}, bf16[1024,2,128]{0,2,1:T(8,128)(2,1)S(1)}, u32[]{:S(2)}, u32[]{:S(2)}) collective-permute-start(bf16[1024,2,128]{0,2,1:T(8,128)(2,1)S(1)} %bitcast_convert_fusion), channel_id=1, source_target_pairs={{0,8},{8,0},{16,24},{24,16},{32,40},{40,32},{48,56},{56,48},{64,72... | collective-permute-start | bytes 1572872 | tf_op jit(solution)/shard_map/ppermute | solution.py:14
  386.5 8.8 %collective-permute-start.2 = (bf16[1024,2]{0,1:T(2,128)(2,1)S(1)}, bf16[1024,2]{0,1:T(2,128)(2,1)S(1)}, u32[]{:S(2)}, u32[]{:S(2)}) collective-permute-start(bf16[1024,2]{0,1:T(2,128)(2,1)S(1)} %bitcast_convert_fusion.2), channel_id=1, source_target_pairs={{0,8},{8,0},{16,24},{24,16},{32,40},{40,32},{48,56},{56,48},{64,72... | collective-permute-start | bytes 12296 | tf_op jit(solution)/shard_map/ppermute | solution.py:14
  389.9 7.4 %collective-permute-start.6 = (bf16[1024,2]{0,1:T(2,128)(2,1)S(1)}, bf16[1024,2]{0,1:T(2,128)(2,1)S(1)}, u32[]{:S(2)}, u32[]{:S(2)}) collective-permute-start(bf16[1024,2]{0,1:T(2,128)(2,1)S(1)} %bitcast_convert_fusion.1), channel_id=1, source_target_pairs={{0,8},{8,0},{16,24},{24,16},{32,40},{40,32},{48,56},{56,48},{64,72... | collective-permute-start | bytes 12296 | tf_op jit(solution)/shard_map/ppermute | solution.py:14
  395.3 4.8 collective-permute-start.4
  400.1 310.7 %copy-start.5 = (f32[256]{0:T(256)S(1)}, f32[256]{0:T(256)}, u32[]{:S(2)}) copy-start(f32[256]{0:T(256)} %param.18) | copy-start | bytes 3076
  401.2 10.9 %collective-permute-start.5 = (bf16[1024,2,128]{0,2,1:T(8,128)(2,1)}, bf16[1024,2,128]{0,2,1:T(8,128)(2,1)S(1)}, u32[]{:S(2)}, u32[]{:S(2)}) collective-permute-start(bf16[1024,2,128]{0,2,1:T(8,128)(2,1)} %get-tuple-element.121), channel_id=1, source_target_pairs={{0,16},{8,24},{16,0},{24,8},{32,48},{40,56},{48,32},{56,40},{64,80... | collective-permute-start | bytes 1572872 | tf_op jit(solution)/shard_map/ppermute | solution.py:14
  403.1 8.9 %collective-permute-start.7 = (bf16[1024,2]{0,1:T(2,128)(2,1)S(1)}, bf16[1024,2]{0,1:T(2,128)(2,1)S(1)}, u32[]{:S(2)}, u32[]{:S(2)}) collective-permute-start(bf16[1024,2]{0,1:T(2,128)(2,1)S(1)} %get-tuple-element.129), channel_id=1, source_target_pairs={{0,16},{8,24},{16,0},{24,8},{32,48},{40,56},{48,32},{56,40},{64,80... | collective-permute-start | bytes 12296 | tf_op jit(solution)/shard_map/ppermute | solution.py:14
Sparse Core Ops, SparseCore 0:
  10.1 40.4 all-gather.3
  52.7 255.5 all-gather.5
  323.4 299.0 all-gather.7
  625.4 85.4 reduce-scatter.1
where the time goes:
time: 720 us; the launch traced here: 719 us
  waiting for transfers between devices  623 us (87%)
  matrix products  28.1 us (4%)
  other arithmetic  24.8 us (3%)
  starting transfers between devices  18.4 us (3%)
  between operations  14.8 us (2%)
    all_gather x1, waiting for transfers between devices, on_device(): lax.all_gather(qkv_weight, 'seq', axis=1, tiled=True)  255 us
    all_gather x1, waiting for transfers between devices, on_device(): lax.all_gather(out_weight, 'seq', axis=1, tiled=True)  210 us
    reduce_scatter x1, waiting for transfers between devices, on_device(): lax.psum_scatter(partial_out.astype(jnp.bfloat16), 'tp', scatter_dimensio...  85.6 us
    all_gather x1, waiting for transfers between devices, on_device(): features_all = lax.all_gather(hidden_in, 'tp', axis=1, tiled=True)  41.9 us
    ppermute x8, waiting for transfers between devices, from_partner(): lax.ppermute(value, axis, [(i, i ^ 1 << bit) for i in range(lax.axis_size...  28.9 us
    ppermute x8, starting transfers between devices, from_partner(): lax.ppermute(value, axis, [(i, i ^ 1 << bit) for i in range(lax.axis_size...  18.2 us
  transfers between devices with their start and end apart: 12, of which 9 were waited for; matrix products, arithmetic and copies ran while one was open for 7% of the time, Pallas kernels for 0%

commit v1 on v0

v1 whole, which is shorter than its diff:
```python
import functools
import math

import jax
import jax.numpy as jnp
import numpy as np
from jax import lax
from jax.experimental import pallas as pl
from jax.experimental.pallas import tpu as pltpu
from jax.sharding import PartitionSpec as P

HEADS = 16
HEAD_DIM = 128
REQS = 16
SPAN = 1024
NX, NY, NZ = 4, 8, 2
TP = 8
ROWS = 256
SLOTS = 2304
LOG2E = 1.4426950408889634
MESH = pl.DeviceIdType.MESH
BF16 = jnp.bfloat16
F32 = jnp.float32
VMEM_SPEC = pl.BlockSpec(memory_space=pltpu.VMEM)
SMEM_SPEC = pl.BlockSpec(memory_space=pltpu.SMEM)


class Node:
    def __init__(self, tree, ox, oy, way, parent):
        self.tree, self.ox, self.oy, self.way, self.parent = tree, ox, oy, way, parent
        self.depth = 0 if parent is None else parent.depth + 1
        self.kids = []
        self.sem = None
        if parent is not None:
            parent.kids.append(self)


def build_tree(tree):
    root = Node(tree, 0, 0, None, None)

    def ring(start, axis, far_up):
        size = (NX, NY)[axis]
        for sign in (1, -1):
            most = size // 2 - (0 if (sign == 1) == far_up else 1)
            node = start
            for _ in range(most):
                step = [0, 0]
                step[axis] = -sign
                node = Node(tree, node.ox + step[0], node.oy + step[1], (axis, sign), node)
                yield node

    first, second = (0, 1) if tree == 0 else (1, 0)
    nodes = [root] + list(ring(root, first, True))
    flip = {}
    for node in list(nodes):
        off = node.ox if first == 0 else node.oy
        nodes += list(ring(node, second, (off % 2 == 0) if first == 1 else off in (0, -1)))
    return nodes


TREES = [build_tree(0), build_tree(1)]
EDGES = []
for _tree in TREES:
    for _node in _tree:
        if _node.parent is not None:
            _node.sem = len(EDGES)
            EDGES.append(_node)
N_EDGES = len(EDGES)
ORDER = sorted(EDGES, key=lambda n: (n.depth, n.sem))


class Place:
    def __init__(self):
        self.s = lax.axis_index("seq")
        self.t = lax.axis_index("tp")
        self.x = lax.div(self.s, NY * NZ)
        self.y = lax.rem(lax.div(self.s, NZ), NY)
        self.z = lax.rem(self.s, NZ)
        self.zh = lax.div(self.t, 2)
        self.core = lax.rem(self.t, 2)

    def seq(self, x, y, z):
        return (x * NY + y) * NZ + z

    def beside(self, axis, sign):
        if axis == 0:
            return (self.seq(lax.rem(self.x + sign + NX, NX), self.y, self.z), self.t)
        return (self.seq(self.x, lax.rem(self.y + sign + NY, NY), self.z), self.t)

    def z_partner(self):
        return (self.seq(self.x, self.y, 1 - self.z), self.t)

    def y_partner(self):
        return (self.seq(self.x, self.y + 1 - 2 * lax.rem(self.y, 2), self.z), self.t)

    def diagonal(self):
        return (self.seq(self.x, self.y + 1 - 2 * lax.rem(self.y, 2), 1 - self.z), self.t)

    def core_partner(self):
        return (self.s, self.zh * 2 + 1 - self.core)

    def up(self, hops):
        return (self.s, lax.rem(self.zh + hops + 4, 4) * 2 + self.core)

    def piece(self, bufs, node):
        ax = lax.rem(self.x + node.ox + NX, NX)
        ay = lax.rem(self.y + node.oy + NY, NY)
        if node.tree == 0:
            return bufs[0].at[ay, ax]
        return bufs[1].at[ax, ay]


def greet(devices):
    barrier = pltpu.get_barrier_semaphore()
    for device in devices:
        pl.semaphore_signal(barrier, inc=1, device_id=device, device_id_type=MESH)
    pl.semaphore_wait(barrier, len(devices))


def remote(src, dst, send_sem, recv_sem, device):
    return pltpu.make_async_remote_copy(
        src_ref=src, dst_ref=dst, send_sem=send_sem, recv_sem=recv_sem,
        device_id=device, device_id_type=MESH,
    )


class Gather:
    def __init__(self, place, halves, bufs, local_sem, zsend, zrecv, send, recv):
        self.p, self.halves, self.bufs = place, halves, bufs
        self.local_sem, self.zsend, self.zrecv, self.send, self.recv = local_sem, zsend, zrecv, send, recv
        self.sent = []

    def own(self, k):
        p = self.p
        return self.bufs[0].at[p.y, p.x, p.z] if k == 0 else self.bufs[1].at[p.x, p.y, p.z]

    def other(self, k):
        p = self.p
        return self.bufs[0].at[p.y, p.x, 1 - p.z] if k == 0 else self.bufs[1].at[p.x, p.y, 1 - p.z]

    def begin(self):
        self.locals = []
        for k in (0, 1):
            copy = remote(self.halves[k], self.own(k), self.zsend.at[k], self.zrecv.at[k], self.p.z_partner())
            copy.start()
            self.sent.append(copy)
        for k in (0, 1):
            copy = pltpu.make_async_copy(self.halves[k], self.own(k), self.local_sem.at[k])
            copy.start()
            self.locals.append(copy)

    def forward(self, node):
        for kid in node.kids:
            piece = self.p.piece(self.bufs, node)
            copy = remote(piece, piece, self.send.at[kid.sem], self.recv.at[kid.sem], self.p.beside(*kid.way))
            copy.start()
            self.sent.append(copy)

    def roots(self):
        for k in (0, 1):
            self.locals[k].wait()
            other = self.other(k)
            remote(other, other, self.zsend.at[k], self.zrecv.at[k], self.p.z_partner()).wait_recv()
            self.forward(TREES[k][0])

    def take(self, node):
        piece = self.p.piece(self.bufs, node)
        way = (node.way[0], -node.way[1])
        remote(piece, piece, self.send.at[node.sem], self.recv.at[node.sem], self.p.beside(*way)).wait_recv()
        self.forward(node)

    def finish(self):
        for copy in self.sent:
            copy.wait_send()


class TpGather:
    def __init__(self, place, src, buf, local_sem, send, recv):
        self.p, self.src, self.buf = place, src, buf
        self.local_sem, self.send, self.recv = local_sem, send, recv
        self.sent = []

    def block(self, hops, mine=True):
        p = self.p
        core = p.core if mine else 1 - p.core
        return self.buf.at[lax.rem(p.zh + hops + 4, 4) * 2 + core]

    def copy(self, src, dst, index, device):
        return remote(src, dst, self.send.at[index], self.recv.at[index], device)

    def start(self, src, dst, index, device):
        copy = self.copy(src, dst, index, device)
        copy.start()
        self.sent.append(copy)

    def begin(self):
        p = self.p
        self.start(self.src, self.block(0), 0, p.up(1))
        self.start(self.src, self.block(0), 1, p.up(-1))
        self.start(self.src, self.block(0), 4, p.core_partner())
        self.local = pltpu.make_async_copy(self.src, self.block(0), self.local_sem)
        self.local.start()

    def near(self):
        p = self.p
        half = ROWS // 2
        low, high = self.block(-1), self.block(1)
        self.copy(low, low, 0, p.up(-1)).wait_recv()
        self.start(low.at[pl.ds(0, half)], low.at[pl.ds(0, half)], 2, p.up(1))
        self.start(low, low, 5, p.core_partner())
        self.copy(high, high, 1, p.up(1)).wait_recv()
        self.start(high.at[pl.ds(half, half)], high.at[pl.ds(half, half)], 3, p.up(-1))
        self.start(high, high, 6, p.core_partner())

    def far(self):
        p = self.p
        half = ROWS // 2
        block = self.block(2)
        lower, upper = block.at[pl.ds(0, half)], block.at[pl.ds(half, half)]
        self.copy(lower, lower, 2, p.up(-1)).wait_recv()
        self.copy(upper, upper, 3, p.up(1)).wait_recv()
        self.start(block, block, 7, p.core_partner())

    def rest(self):
        self.local.wait()
        for index, hops in ((4, 0), (5, -1), (6, 1), (7, 2)):
            block = self.block(hops, mine=False)
            self.copy(block, block, index, self.p.core_partner()).wait_recv()

    def finish(self):
        for copy in self.sent:
            copy.wait_send()


def weight_rows(a_ref, b_ref, seqs, pick):
    parts = []
    for s in seqs:
        x, y, z = s // (NY * NZ), (s // NZ) % NY, s % NZ
        parts.append(a_ref[(y, x, z) + pick])
        parts.append(b_ref[(x, y, z) + pick])
    return jnp.concatenate(parts, axis=0)


def project_kernel(
    hidden_ref, gain_ref, shift_ref, weight_ref, bias_ref, out_ref,
    hid, wa, wb, norm,
    local_sem, zsend, zrecv, send, recv, hsend, hrecv,
):
    p = Place()
    greet([p.z_partner(), p.core_partner(), p.up(1), p.up(-1),
           p.beside(0, 1), p.beside(0, -1), p.beside(1, 1), p.beside(1, -1)])
    half = weight_ref.shape[1] // 2
    halves = [weight_ref.at[:, pl.ds(0, half)], weight_ref.at[:, pl.ds(half, half)]]
    weights = Gather(p, halves, (wa, wb), local_sem, zsend, zrecv, send, recv)
    tokens = TpGather(p, hidden_ref, hid, local_sem.at[2], hsend, hrecv)
    weights.begin()
    tokens.begin()
    weights.roots()

    def normalise(first, rows):
        values = [hid[t, first:first + rows, :].astype(F32) for t in range(TP)]
        total = functools.reduce(jnp.add, values)
        mean = jnp.sum(total, axis=1, keepdims=True) * (1.0 / (TP * ROWS))
        values = [v - mean for v in values]
        squares = functools.reduce(jnp.add, [v * v for v in values])
        variance = jnp.sum(squares, axis=1, keepdims=True) * (1.0 / (TP * ROWS))
        scale = lax.rsqrt(variance + 1e-05)
        for t in range(TP):
            norm[t, first:first + rows, :] = (values[t] * scale * gain_ref[t] + shift_ref[t]).astype(BF16)

    depth = 0
    for node in ORDER:
        if node.depth != depth:
            depth = node.depth
            if depth == 2:
                tokens.near()
            elif depth == 3:
                tokens.far()
            elif depth == 4:
                tokens.rest()
            elif depth == 5:
                normalise(0, 128)
            elif depth == 6:
                normalise(128, 128)
        weights.take(node)
    for index in range(3):
        total = None
        for t in range(TP):
            rows = weight_rows(wa, wb, range(t * 8, t * 8 + 8), (index,))
            part = jnp.dot(norm[t], rows, preferred_element_type=F32)
            total = part if total is None else total + part
        total = total + bias_ref[index]
        if index == 0:
            total = total * (LOG2E / math.sqrt(HEAD_DIM))
        out_ref[index] = total.astype(BF16)
    weights.finish()
    tokens.finish()


def share_kernel(
    qkv_ref, out_weight_ref, all_ref, oa_ref, ob_ref,
    local_sem, zsend, zrecv, send, recv, gsend, grecv,
):
    p = Place()
    greet([p.z_partner(), p.y_partner(), p.diagonal(),
           p.beside(0, 1), p.beside(0, -1), p.beside(1, 1), p.beside(1, -1)])
    half = out_weight_ref.shape[0] // 2
    halves = [out_weight_ref.at[pl.ds(0, half)], out_weight_ref.at[pl.ds(half, half)]]
    weights = Gather(p, halves, (oa_ref, ob_ref), local_sem, zsend, zrecv, send, recv)
    local = lax.rem(p.s, 4)
    slot = all_ref.at[local]
    sent = []
    peers = [p.y_partner(), p.z_partner(), p.diagonal()]
    for index, peer in enumerate(peers):
        copy = remote(qkv_ref, slot, gsend.at[index], grecv.at[index], peer)
        copy.start()
        sent.append(copy)
    weights.begin()
    mine = pltpu.make_async_copy(qkv_ref, slot, local_sem.at[2])
    mine.start()
    weights.roots()
    for node in ORDER:
        weights.take(node)
    for index, peer in enumerate(peers):
        theirs = all_ref.at[lax.rem(peer[0], 4)]
        remote(theirs, theirs, gsend.at[index], grecv.at[index], peer).wait_recv()
    mine.wait()
    weights.finish()
    for copy in sent:
        copy.wait_send()


def attend_kernel(
    numbers_ref, q_ref, keys_ref, values_ref, fresh_ref, bias_ref, out_ref, lse_ref, kaug, vaug,
):
    block = pl.program_id(0)
    first, local = numbers_ref[0], numbers_ref[1]

    @pl.when(block == 0)
    def _():
        def aux(count, start, live_only):
            place = lax.broadcasted_iota(jnp.int32, (count, HEAD_DIM), 0) + start
            lane = lax.broadcasted_iota(jnp.int32, (count, HEAD_DIM), 1)
            high = lax.shift_right_arithmetic(place, 7)
            low = place - high * 128
            number = jnp.where(lane < 3, high, jnp.where(lane < 6, low, 0)).astype(F32)
            if live_only:
                dead = place >= 0
                number = jnp.where(dead, jnp.where(lane == 6, -1e30, 0.0), number)
            return number.astype(BF16)

        cached = aux(SLOTS, first, True)
        fresh = aux(ROWS, local * ROWS, False)
        alive = lax.broadcasted_iota(jnp.int32, (SLOTS, HEAD_DIM), 0) + first < 0
        one = lax.broadcasted_iota(jnp.int32, (SLOTS, HEAD_DIM), 1) == 0
        ones = jnp.where(one, 1.0, 0.0).astype(BF16)
        for head in range(2):
            cols = slice(head * HEAD_DIM, (head + 1) * HEAD_DIM)
            kaug[head, :SLOTS, :HEAD_DIM] = jnp.where(alive, keys_ref[:, cols].astype(F32), 0.0).astype(BF16)
            kaug[head, :SLOTS, HEAD_DIM:] = cached
            kaug[head, SLOTS:, :HEAD_DIM] = fresh_ref[1, :, cols]
            kaug[head, SLOTS:, HEAD_DIM:] = fresh
            vaug[head, :SLOTS, :HEAD_DIM] = values_ref[:, cols]
            vaug[head, :SLOTS, HEAD_DIM:] = ones
            vaug[head, SLOTS:, :HEAD_DIM] = fresh_ref[2, :, cols]
            vaug[head, SLOTS:, HEAD_DIM:] = ones[:ROWS]

    row = lax.broadcasted_iota(jnp.int32, (ROWS, ROWS), 0) + block * ROWS
    column = lax.broadcasted_iota(jnp.int32, (ROWS, ROWS), 1) + local * ROWS
    lses = []
    for head in range(2):
        cols = slice(head * HEAD_DIM, (head + 1) * HEAD_DIM)
        bias = jnp.broadcast_to(bias_ref[head].astype(F32), (ROWS, HEAD_DIM)).astype(BF16)
        query = jnp.concatenate([q_ref[0, 0, :, cols], bias], axis=1)
        nt = (((1,), (1,)), ((), ()))
        cached = lax.dot_general(query, kaug[head, :SLOTS], nt, preferred_element_type=F32)
        fresh = lax.dot_general(query, kaug[head, SLOTS:], nt, preferred_element_type=F32)
        fresh = jnp.where(column <= row, fresh, -1e30)
        top = jnp.maximum(
            jnp.max(cached, axis=1, keepdims=True), jnp.max(fresh, axis=1, keepdims=True)
        )
        weight_c = jnp.exp2(cached - top).astype(BF16)
        weight_f = jnp.exp2(fresh - top).astype(BF16)
        both = jnp.dot(weight_c, vaug[head, :SLOTS], preferred_element_type=F32)
        both += jnp.dot(weight_f, vaug[head, SLOTS:], preferred_element_type=F32)
        total = both[:, HEAD_DIM:HEAD_DIM + 1]
        out_ref[0, :, cols] = (both[:, :HEAD_DIM] / total).astype(BF16)
        lses.append(top + jnp.log2(total))
    lane = lax.broadcasted_iota(jnp.int32, (ROWS, HEAD_DIM), 1)
    side = jnp.where(lane == 0, lses[0], lses[1])
    lse_ref[0] = jnp.transpose(side)[:8]


def output_kernel(
    part_ref, lse_ref, oa_ref, ob_ref, bias_ref, out_ref,
    parts, sides, mine, att, local_sem, psend, precv, tsend, trecv,
):
    p = Place()
    peers = [p.y_partner(), p.z_partner(), p.diagonal()]
    greet(peers + [p.core_partner(), p.up(1), p.up(-1)])
    local = lax.rem(p.s, 4)
    sent = []
    for index, peer in enumerate(peers):
        theirs = lax.rem(peer[0], 4)
        for copy in (
            remote(part_ref.at[theirs], parts.at[local], psend.at[index], precv.at[index], peer),
            remote(lse_ref.at[theirs], sides.at[local], psend.at[3 + index], precv.at[3 + index], peer),
        ):
            copy.start()
            sent.append(copy)
    own = [
        pltpu.make_async_copy(part_ref.at[local], parts.at[local], local_sem.at[1]),
        pltpu.make_async_copy(lse_ref.at[local], sides.at[local], local_sem.at[2]),
    ]
    for copy in own:
        copy.start()
    for copy in own:
        copy.wait()
    for index, peer in enumerate(peers):
        theirs = lax.rem(peer[0], 4)
        a, b = parts.at[theirs], sides.at[theirs]
        remote(a, a, psend.at[index], precv.at[index], peer).wait_recv()
        remote(b, b, psend.at[3 + index], precv.at[3 + index], peer).wait_recv()
    stats = [sides[k] for k in range(4)]
    top = functools.reduce(jnp.maximum, stats)
    shares = [jnp.exp2(stat - top) for stat in stats]
    total = functools.reduce(jnp.add, shares)
    shares = [jnp.transpose(jnp.concatenate([share / total] * 16, axis=0)) for share in shares]
    for head in range(2):
        cols = slice(head * HEAD_DIM, (head + 1) * HEAD_DIM)
        terms = [parts[k, :, cols].astype(F32) * shares[k][:, head:head + 1] for k in range(4)]
        mine[:, cols] = functools.reduce(jnp.add, terms).astype(BF16)
    gather = TpGather(p, mine, att, local_sem.at[0], tsend, trecv)
    gather.begin()
    gather.near()
    gather.far()
    gather.rest()
    result = None
    for t in range(TP):
        rows = weight_rows(oa_ref, ob_ref, range(t, 64, TP), ())
        term = lax.dot_general(att[t], rows, (((1,), (1,)), ((), ())), preferred_element_type=F32)
        result = term if result is None else result + term
    out_ref[...] = (result + bias_ref[...]).astype(BF16)
    gather.finish()
    for copy in sent:
        copy.wait_send()


PAD = ROWS + 32


def cache_kernel(numbers_ref, all_ref, keys_ref, values_ref, keys_out, values_out, fresh):
    step = pl.program_id(0)

    @pl.when(step == 0)
    def _():
        for k in range(2):
            for h in range(2):
                fresh[2 * k + h, :PAD] = jnp.zeros((PAD, HEAD_DIM), F32)
                fresh[2 * k + h, PAD + SPAN:] = jnp.zeros((PAD, HEAD_DIM), F32)
                for block in range(4):
                    rows = all_ref[block, 1 + k, :, h * HEAD_DIM:(h + 1) * HEAD_DIM]
                    fresh[2 * k + h, PAD + block * ROWS:PAD + (block + 1) * ROWS] = rows.astype(F32)

    start = step * ROWS + numbers_ref[0]
    touched = (start > -ROWS) & (start < SPAN)

    @pl.when(touched)
    def _():
        begin = jnp.clip(start, -ROWS, SPAN)
        place = lax.broadcasted_iota(jnp.int32, (ROWS, HEAD_DIM), 0) + begin
        inside = (place >= 0) & (place < SPAN)
        for k, (old, new) in enumerate(((keys_ref, keys_out), (values_ref, values_out))):
            for h in range(2):
                cols = slice(h * HEAD_DIM, (h + 1) * HEAD_DIM)
                rows = fresh[2 * k + h, pl.ds(begin + PAD, ROWS), :]
                new[:, cols] = jnp.where(inside, rows, old[:, cols].astype(F32)).astype(BF16)

    @pl.when(jnp.logical_not(touched))
    def _():
        keys_out[...] = keys_ref[...]
        values_out[...] = values_ref[...]


def round_bf16(value):
    return np.asarray(np.asarray(value, np.float32).astype(jnp.bfloat16), np.float64)


def bias_table():
    table = np.zeros((HEADS, 1, HEAD_DIM), np.float64)
    for head in range(HEADS):
        slope = 2.0 ** (-8.0 * (head + 1) / HEADS) * LOG2E
        for column, value in ((0, slope * 128.0), (3, slope)):
            rest = value
            for k in range(3):
                table[head, 0, column + k] = round_bf16(rest)
                rest = rest - table[head, 0, column + k]
        table[head, 0, 6] = 1.0
    return table.astype(np.float32)


def remote_params(ident):
    return pltpu.CompilerParams(collective_id=ident, has_side_effects=True, vmem_limit_bytes=48 << 20)


def dma(*count):
    return pltpu.SemaphoreType.DMA(count)


def on_device(
    hidden_in, norm_gain, norm_bias, qkv_weight, qkv_bias, out_weight, out_bias, key_cache, value_cache, cached_len,
):
    moves = []
    for s in range(64):
        for t in range(TP):
            moves.append((s * TP + t, ((s % 8) * 8 + t) * TP + s // 8))
    out_block = lax.ppermute(out_weight.T, ("seq", "tp"), moves)

    qkv = pl.pallas_call(
        project_kernel,
        name="project",
        out_shape=jax.ShapeDtypeStruct((3, ROWS, ROWS), BF16),
        in_specs=[VMEM_SPEC] * 5,
        out_specs=VMEM_SPEC,
        scratch_shapes=[
            pltpu.VMEM((TP, ROWS, ROWS), BF16),
            pltpu.VMEM((NY, NX, NZ, 3, 16, ROWS), BF16),
            pltpu.VMEM((NX, NY, NZ, 3, 16, ROWS), BF16),
            pltpu.VMEM((TP, ROWS, ROWS), BF16),
            dma(3), dma(2), dma(2), dma(N_EDGES), dma(N_EDGES), dma(8), dma(8),
        ],
        compiler_params=remote_params(0),
    )(
        hidden_in, norm_gain.reshape(TP, 1, ROWS), norm_bias.reshape(TP, 1, ROWS),
        qkv_weight, qkv_bias.reshape(3, 1, ROWS),
    )

    shared, oa, ob = pl.pallas_call(
        share_kernel,
        name="share",
        out_shape=(
            jax.ShapeDtypeStruct((4, 3, ROWS, ROWS), BF16),
            jax.ShapeDtypeStruct((NY, NX, NZ, 16, ROWS), BF16),
            jax.ShapeDtypeStruct((NX, NY, NZ, 16, ROWS), BF16),
        ),
        in_specs=[VMEM_SPEC] * 2,
        out_specs=(VMEM_SPEC,) * 3,
        scratch_shapes=[dma(3), dma(2), dma(2), dma(N_EDGES), dma(N_EDGES), dma(3), dma(3)],
        compiler_params=remote_params(1),
    )(qkv, out_block)

    seq_index = lax.axis_index("seq")
    local = seq_index % 4
    length = lax.dynamic_index_in_dim(cached_len, seq_index // 4, 0, keepdims=False)
    numbers = jnp.stack([local * SLOTS - length, local]).astype(jnp.int32)
    bias = lax.dynamic_slice_in_dim(jnp.asarray(bias_table()), lax.axis_index("tp") * 2, 2, 0)

    part, lse = pl.pallas_call(
        attend_kernel,
        name="attend",
        grid=(4,),
        out_shape=(
            jax.ShapeDtypeStruct((4, ROWS, ROWS), BF16),
            jax.ShapeDtypeStruct((4, 8, ROWS), F32),
        ),
        in_specs=[
            SMEM_SPEC,
            pl.BlockSpec((1, 1, ROWS, ROWS), lambda j: (j, 0, 0, 0)),
            VMEM_SPEC, VMEM_SPEC, VMEM_SPEC, VMEM_SPEC,
        ],
        out_specs=(
            pl.BlockSpec((1, ROWS, ROWS), lambda j: (j, 0, 0)),
            pl.BlockSpec((1, 8, ROWS), lambda j: (j, 0, 0)),
        ),
        scratch_shapes=[
            pltpu.VMEM((2, SLOTS + ROWS, ROWS), BF16),
            pltpu.VMEM((2, SLOTS + ROWS, ROWS), BF16),
        ],
        compiler_params=pltpu.CompilerParams(vmem_limit_bytes=48 << 20),
    )(numbers, shared, key_cache, value_cache, qkv, bias)

    mixed = pl.pallas_call(
        output_kernel,
        name="output",
        out_shape=jax.ShapeDtypeStruct((ROWS, ROWS), BF16),
        in_specs=[VMEM_SPEC] * 5,
        out_specs=VMEM_SPEC,
        scratch_shapes=[
            pltpu.VMEM((4, ROWS, ROWS), BF16),
            pltpu.VMEM((4, 8, ROWS), F32),
            pltpu.VMEM((ROWS, ROWS), BF16),
            pltpu.VMEM((TP, ROWS, ROWS), BF16),
            dma(3), dma(6), dma(6), dma(8), dma(8),
        ],
        compiler_params=remote_params(2),
    )(part, lse, oa, ob, out_bias.reshape(1, ROWS))

    block = pl.BlockSpec((ROWS, ROWS), lambda j: (j, 0))
    keys_new, values_new = pl.pallas_call(
        cache_kernel,
        name="cache",
        grid=(SLOTS // ROWS,),
        out_shape=(jax.ShapeDtypeStruct((SLOTS, ROWS), BF16),) * 2,
        in_specs=[SMEM_SPEC, VMEM_SPEC, block, block],
        out_specs=(block, block),
        scratch_shapes=[pltpu.VMEM((4, SPAN + 2 * PAD, HEAD_DIM), F32)],
        compiler_params=pltpu.CompilerParams(vmem_limit_bytes=32 << 20),
    )(numbers, shared, key_cache, value_cache)
    return (mixed, keys_new, values_new)


def solution(mesh):
    placed = (
        P("seq", "tp"),
        P(),
        P(),
        P(None, "seq", "tp"),
        P(None, "tp"),
        P("tp", "seq"),
        P("tp"),
        P("seq", "tp"),
        P("seq", "tp"),
        P(),
    )
    return jax.shard_map(
        on_device,
        mesh=mesh,
        in_specs=placed,
        out_specs=(P("seq", "tp"), P("seq", "tp"), P("seq", "tp")),
        check_vma=False,
    )
```

time: 720 us -> 149 us (0.21)
  waiting for transfers between devices: 623 us -> 0.01 us
  Pallas kernels: 0 us -> 133 us
  matrix products: 28.1 us -> 0 us
  other arithmetic: 24.8 us -> 0.07 us
  between operations: 14.8 us -> 1.37 us
  starting transfers between devices: 18.4 us -> 5.38 us
    all_gather x3 -> x0, waiting for transfers between devices: 507 us -> none  [the longest x1 255 us: on_device(): lax.all_gather(qkv_weight, 'seq', axis=1, tiled=True)]
    pallas_call x0 -> x5, Pallas kernels: none -> 133 us  [the longest x1 47.4 us: on_device(): pl.pallas_call(project_kernel, name='project', out_shape=jax.ShapeDtypeSt...]
    reduce_scatter x1 -> x0, waiting for transfers between devices: 85.6 us -> none  [on_device(): lax.psum_scatter(partial_out.astype(jnp.bfloat16), 'tp', scatter_dimensio...]
    ppermute x8 -> x1, waiting for transfers between devices: 28.9 us -> 0.01 us  [on_device(): out_block = lax.ppermute(out_weight.T, ('seq', 'tp'), moves)]
    dot_general x6 -> x0, matrix products: 28.1 us -> none  [the longest x2 13.3 us: one_head(): jnp.dot(weights.astype(jnp.bfloat16), value_one, preferred_element_type=j...]
    ppermute x8 -> x1, starting transfers between devices: 18.2 us -> 5.38 us  [on_device(): out_block = lax.ppermute(out_weight.T, ('seq', 'tp'), moves)]
    reduce_sum x4 -> x0, other arithmetic: 12.2 us -> none  [the longest x2 9.15 us: one_head(): totals = jnp.sum(weights, axis=1)]
  transfers between devices with their start and end apart: 12 -> 1, of which waited for: 9 -> 0; matrix products, arithmetic and copies ran while one was open for 7% -> 2% of each run, Pallas kernels for 0% -> 32%
where the time goes in v1:
time: 149 us
  Pallas kernels  133 us (89%)
  local copies, waits for them, and re-layouts  8.92 us (6%)
  starting transfers between devices  5.38 us (4%)
    pallas_call x1, Pallas kernels, on_device(): pl.pallas_call(project_kernel, name='project', out_shape=jax.ShapeDtypeSt...  47.4 us
    pallas_call x1, Pallas kernels, on_device(): pl.pallas_call(output_kernel, name='output', out_shape=jax.ShapeDtypeStru...  36.4 us
    pallas_call x1, Pallas kernels, on_device(): pl.pallas_call(share_kernel, name='share', out_shape=(jax.ShapeDtypeStruc...  32.4 us
    pallas_call x1, Pallas kernels, on_device(): pl.pallas_call(attend_kernel, name='attend', grid=(4,), out_shape=(jax.Sh...  12.1 us
    unnamed x19, local copies, waits for them, and re-layouts  6.3 us
    ppermute x1, starting transfers between devices, on_device(): out_block = lax.ppermute(out_weight.T, ('seq', 'tp'), moves)  5.38 us
    pallas_call x1, Pallas kernels, on_device(): pl.pallas_call(cache_kernel, name='cache', grid=(SLOTS // ROWS,), out_sha...  4.57 us
  transfers between devices with their start and end apart: 1, of which 0 were waited for; matrix products, arithmetic and copies ran while one was open for 2% of the time, Pallas kernels for 32%

profile of v1, /device:TPU:1, one launch (start us, length us, event | category | flops | bytes accessed | tf_op | source)
XLA Modules:
  0.0 148.6 jit_solution(16657529644316458176)
XLA Ops:
  0.6 5.4 %collective-permute-start = (bf16[32,256]{1,0:T(8,128)(2,1)}, bf16[32,256]{1,0:T(8,128)(2,1)S(1)}, u32[]{:S(2)}, u32[]{:S(2)}) collective-permute-start(bf16[32,256]{1,0:T(8,128)(2,1)} %bitcast.10), channel_id=1, source_target_pairs={{0,0},{1,8},{2,16},{3,24},{4,32},{5,40},{6,48},{7,56},{8,64},{9,72... | collective-permute-start | bytes 49160 | tf_op jit(solution)/shard_map/ppermute | solution.py:517
  6.0 1.2 dynamic_slice.7
  7.9 0.7 constant_dynamic-slice_fusion.bias_ref
  8.6 0.1 pad_add_fusion.numbers_ref
  8.7 0.7 reshape.20.bias_ref
  9.4 0.0 copy-start.4
  9.4 0.9 copy-done.4
  10.3 0.0 copy-start.5
  10.3 0.8 copy-done.5
  11.1 0.7 copy-done.6
  11.8 0.7 copy-done.7
  12.5 47.4 %project.1.qkv_ref.fresh_ref = bf16[3,256,256]{2,1,0:T(8,128)(2,1)S(1)} custom-call(bf16[256,256]{1,0:T(8,128)(2,1)S(1)} %copy-done.4, f32[8,1,256]{2,1,0:T(1,128)S(1)} %bitcast.7, f32[8,1,256]{2,1,0:T(1,128)S(1)} %bitcast.8, bf16[3,32,256]{2,1,0:T(8,128)(2,1)S(1)} %copy-done.5, f32[3,1,256]{2,1,0:T(1,128)S(1)} %reshape.20.bias_ref), custom_call_target="tpu_custom_call" | custom-call | tf_op jit(solution)/shard_map/project/pallas_call | solution.py:519
  59.9 0.0 collective-permute-done.out_weight_ref
  59.9 32.4 %share.1 = (bf16[4,3,256,256]{3,2,1,0:T(8,128)(2,1)S(1)}, bf16[8,4,2,16,256]{4,3,2,1,0:T(8,128)(2,1)S(1)}, bf16[4,8,2,16,256]{4,3,2,1,0:T(8,128)(2,1)S(1)}) custom-call(bf16[3,256,256]{2,1,0:T(8,128)(2,1)S(1)} %project.1.qkv_ref.fresh_ref, bf16[32,256]{1,0:T(8,128)(2,1)S(1)} %collective-permute-done.out_weight_ref), custom_call_target="tpu_custom_call" | custom-call | tf_op jit(solution)/shard_map/share/pallas_call | solution.py:538
  92.3 0.0 copy-start
  92.3 1.3 copy-done
  93.6 1.3 copy-done.2
  94.9 4.6 %cache.1 = (bf16[2304,256]{1,0:T(8,128)(2,1)}, bf16[2304,256]{1,0:T(8,128)(2,1)}) custom-call(s32[2]{0:T(128)S(1)} %pad_add_fusion.numbers_ref, bf16[4,3,256,256]{3,2,1,0:T(8,128)(2,1)S(1)} %get-tuple-element.10.q_ref.all_ref, bf16[2304,256]{1,0:T(8,128)(2,1)S(1)} %copy-done, bf16[2304,256]{1,0:T(8,128)(2,1)S(1)} %copy-done.2), custom_call_target="tpu_custom_call" | custom-call | tf_op jit(solution)/shard_map/cache/pallas_call | solution.py:599
  99.4 0.0 copy-done.1
  99.4 0.0 copy-done.3
  99.5 12.1 %attend.1 = (bf16[4,256,256]{2,1,0:T(8,128)(2,1)S(1)}, f32[4,8,256]{2,1,0:T(8,128)S(1)}) custom-call(s32[2]{0:T(128)S(1)} %pad_add_fusion.numbers_ref, bf16[4,3,256,256]{3,2,1,0:T(8,128)(2,1)S(1)} %get-tuple-element.10.q_ref.all_ref, bf16[2304,256]{1,0:T(8,128)(2,1)S(1)} %copy-done.1, bf16[2304,256]{1,0:T(8,128)(2,1)S(1)} %copy-done.3, ...), custom_call_target="tpu_custom_call" | custom-call | tf_op jit(solution)/shard_map/attend/pallas_call | solution.py:558
  111.6 0.0 copy-done.8
  111.6 36.4 %output.1 = bf16[256,256]{1,0:T(8,128)(2,1)S(1)} custom-call(bf16[4,256,256]{2,1,0:T(8,128)(2,1)S(1)} %get-tuple-element.11.part_ref, f32[4,8,256]{2,1,0:T(8,128)S(1)} %get-tuple-element.12.lse_ref, bf16[8,4,2,16,256]{4,3,2,1,0:T(8,128)(2,1)S(1)} %get-tuple-element.13.oa_ref, bf16[4,8,2,16,256]{4,3,2,1,0:T(8,128)(2,1)S(1)} %get-tuple-element.14.ob_ref, ...), custom_call_target="tpu_custom_call" | custom-call | tf_op jit(solution)/shard_map/output/pallas_call | solution.py:582
  148.0 0.7 copy.15
  (6 shorter events, 0.0 us)
Async XLA Ops:
  0.6 59.3 %collective-permute-start = (bf16[32,256]{1,0:T(8,128)(2,1)}, bf16[32,256]{1,0:T(8,128)(2,1)S(1)}, u32[]{:S(2)}, u32[]{:S(2)}) collective-permute-start(bf16[32,256]{1,0:T(8,128)(2,1)} %bitcast.10), channel_id=1, source_target_pairs={{0,0},{1,8},{2,16},{3,24},{4,32},{5,40},{6,48},{7,56},{8,64},{9,72... | collective-permute-start | bytes 49160 | tf_op jit(solution)/shard_map/ppermute | solution.py:517
  9.4 0.9 copy-start.4
  10.3 0.8 copy-start.5
  11.1 0.7 copy-start.6
  11.8 0.7 copy-start.7
  92.3 1.3 copy-start
  93.6 1.3 copy-start.2
  94.9 4.6 %copy-start.1 = (bf16[2304,256]{1,0:T(8,128)(2,1)S(1)}, bf16[2304,256]{1,0:T(8,128)(2,1)}, u32[]{:S(2)}) copy-start(bf16[2304,256]{1,0:T(8,128)(2,1)} %keys_ref.3) | copy-start | bytes 3538948
  94.9 4.6 %copy-start.3 = (bf16[2304,256]{1,0:T(8,128)(2,1)S(1)}, bf16[2304,256]{1,0:T(8,128)(2,1)}, u32[]{:S(2)}) copy-start(bf16[2304,256]{1,0:T(8,128)(2,1)} %values_ref.3) | copy-start | bytes 3538948
  99.5 12.1 %copy-start.8 = (f32[256]{0:T(256)S(1)}, f32[256]{0:T(256)}, u32[]{:S(2)}) copy-start(f32[256]{0:T(256)} %param.17) | copy-start | bytes 3076

commit v2 on v1

v2 whole, which is shorter than its diff:
```python
import functools
import math

import jax
import jax.numpy as jnp
import numpy as np
from jax import lax
from jax.experimental import pallas as pl
from jax.experimental.pallas import tpu as pltpu
from jax.sharding import PartitionSpec as P

HEADS = 16
HEAD_DIM = 128
REQS = 16
SPAN = 1024
NX, NY, NZ = 4, 8, 2
TP = 8
ROWS = 256
SLOTS = 2304
LOG2E = 1.4426950408889634
MESH = pl.DeviceIdType.MESH
BF16 = jnp.bfloat16
F32 = jnp.float32
VMEM_SPEC = pl.BlockSpec(memory_space=pltpu.VMEM)
SMEM_SPEC = pl.BlockSpec(memory_space=pltpu.SMEM)


class Node:
    def __init__(self, tree, ox, oy, way, parent):
        self.tree, self.ox, self.oy, self.way, self.parent = tree, ox, oy, way, parent
        self.depth = 0 if parent is None else parent.depth + 1
        self.kids = []
        self.sem = None
        if parent is not None:
            parent.kids.append(self)


def build_tree(tree):
    root = Node(tree, 0, 0, None, None)

    def ring(start, axis, far_up):
        size = (NX, NY)[axis]
        for sign in (1, -1):
            most = size // 2 - (0 if (sign == 1) == far_up else 1)
            node = start
            for _ in range(most):
                step = [0, 0]
                step[axis] = -sign
                node = Node(tree, node.ox + step[0], node.oy + step[1], (axis, sign), node)
                yield node

    first, second = (0, 1) if tree == 0 else (1, 0)
    nodes = [root] + list(ring(root, first, True))
    flip = {}
    for node in list(nodes):
        off = node.ox if first == 0 else node.oy
        nodes += list(ring(node, second, (off % 2 == 0) if first == 1 else off in (0, -1)))
    return nodes


TREES = [build_tree(0), build_tree(1)]
EDGES = []
for _tree in TREES:
    for _node in _tree:
        if _node.parent is not None:
            _node.sem = len(EDGES)
            EDGES.append(_node)
N_EDGES = len(EDGES)
ORDER = sorted(EDGES, key=lambda n: (n.depth, n.sem))


class Place:
    def __init__(self):
        self.s = lax.axis_index("seq")
        self.t = lax.axis_index("tp")
        self.x = lax.div(self.s, NY * NZ)
        self.y = lax.rem(lax.div(self.s, NZ), NY)
        self.z = lax.rem(self.s, NZ)
        self.zh = lax.div(self.t, 2)
        self.core = lax.rem(self.t, 2)

    def seq(self, x, y, z):
        return (x * NY + y) * NZ + z

    def beside(self, axis, sign):
        if axis == 0:
            return (self.seq(lax.rem(self.x + sign + NX, NX), self.y, self.z), self.t)
        return (self.seq(self.x, lax.rem(self.y + sign + NY, NY), self.z), self.t)

    def z_partner(self):
        return (self.seq(self.x, self.y, 1 - self.z), self.t)

    def y_partner(self):
        return (self.seq(self.x, self.y + 1 - 2 * lax.rem(self.y, 2), self.z), self.t)

    def diagonal(self):
        return (self.seq(self.x, self.y + 1 - 2 * lax.rem(self.y, 2), 1 - self.z), self.t)

    def core_partner(self):
        return (self.s, self.zh * 2 + 1 - self.core)

    def up(self, hops):
        return (self.s, lax.rem(self.zh + hops + 4, 4) * 2 + self.core)

    def piece(self, bufs, node):
        ax = lax.rem(self.x + node.ox + NX, NX)
        ay = lax.rem(self.y + node.oy + NY, NY)
        if node.tree == 0:
            return bufs[0].at[ay, ax]
        return bufs[1].at[ax, ay]


def remote(src, dst, send_sem, recv_sem, device):
    return pltpu.make_async_remote_copy(
        src_ref=src, dst_ref=dst, send_sem=send_sem, recv_sem=recv_sem,
        device_id=device, device_id_type=MESH,
    )


class Gather:
    def __init__(self, place, halves, bufs, local_sem, zsend, zrecv, send, recv):
        self.p, self.halves, self.bufs = place, halves, bufs
        self.local_sem, self.zsend, self.zrecv, self.send, self.recv = local_sem, zsend, zrecv, send, recv
        self.sent = []

    def own(self, k):
        p = self.p
        return self.bufs[0].at[p.y, p.x, p.z] if k == 0 else self.bufs[1].at[p.x, p.y, p.z]

    def other(self, k):
        p = self.p
        return self.bufs[0].at[p.y, p.x, 1 - p.z] if k == 0 else self.bufs[1].at[p.x, p.y, 1 - p.z]

    def begin(self):
        self.locals = []
        for k in (0, 1):
            src = self.own(k) if self.halves is None else self.halves[k]
            copy = remote(src, self.own(k), self.zsend.at[k], self.zrecv.at[k], self.p.z_partner())
            copy.start()
            self.sent.append(copy)
        if self.halves is None:
            return
        for k in (0, 1):
            copy = pltpu.make_async_copy(self.halves[k], self.own(k), self.local_sem.at[k])
            copy.start()
            self.locals.append(copy)

    def forward(self, node):
        for kid in node.kids:
            piece = self.p.piece(self.bufs, node)
            copy = remote(piece, piece, self.send.at[kid.sem], self.recv.at[kid.sem], self.p.beside(*kid.way))
            copy.start()
            self.sent.append(copy)

    def roots(self):
        for k in (0, 1):
            if self.locals:
                self.locals[k].wait()
            other = self.other(k)
            remote(other, other, self.zsend.at[k], self.zrecv.at[k], self.p.z_partner()).wait_recv()
            self.forward(TREES[k][0])

    def take(self, node):
        piece = self.p.piece(self.bufs, node)
        way = (node.way[0], -node.way[1])
        remote(piece, piece, self.send.at[node.sem], self.recv.at[node.sem], self.p.beside(*way)).wait_recv()
        self.forward(node)

    def finish(self):
        for copy in self.sent:
            copy.wait_send()


class TpGather:
    def __init__(self, place, src, buf, local_sem, send, recv):
        self.p, self.src, self.buf = place, src, buf
        self.local_sem, self.send, self.recv = local_sem, send, recv
        self.sent = []

    def block(self, hops, mine=True):
        p = self.p
        core = p.core if mine else 1 - p.core
        return self.buf.at[lax.rem(p.zh + hops + 4, 4) * 2 + core]

    def copy(self, src, dst, index, device):
        return remote(src, dst, self.send.at[index], self.recv.at[index], device)

    def start(self, src, dst, index, device):
        copy = self.copy(src, dst, index, device)
        copy.start()
        self.sent.append(copy)

    def begin(self):
        p = self.p
        self.start(self.src, self.block(0), 0, p.up(1))
        self.start(self.src, self.block(0), 1, p.up(-1))
        self.start(self.src, self.block(0), 4, p.core_partner())
        self.local = pltpu.make_async_copy(self.src, self.block(0), self.local_sem)
        self.local.start()

    def near(self):
        p = self.p
        half = ROWS // 2
        low, high = self.block(-1), self.block(1)
        self.copy(low, low, 0, p.up(-1)).wait_recv()
        self.start(low.at[pl.ds(0, half)], low.at[pl.ds(0, half)], 2, p.up(1))
        self.start(low, low, 5, p.core_partner())
        self.copy(high, high, 1, p.up(1)).wait_recv()
        self.start(high.at[pl.ds(half, half)], high.at[pl.ds(half, half)], 3, p.up(-1))
        self.start(high, high, 6, p.core_partner())

    def far(self):
        p = self.p
        half = ROWS // 2
        block = self.block(2)
        lower, upper = block.at[pl.ds(0, half)], block.at[pl.ds(half, half)]
        self.copy(lower, lower, 2, p.up(-1)).wait_recv()
        self.copy(upper, upper, 3, p.up(1)).wait_recv()
        self.start(block, block, 7, p.core_partner())

    def rest(self):
        self.local.wait()
        for index, hops in ((4, 0), (5, -1), (6, 1), (7, 2)):
            block = self.block(hops, mine=False)
            self.copy(block, block, index, self.p.core_partner()).wait_recv()

    def finish(self):
        for copy in self.sent:
            copy.wait_send()


def weight_rows(a_ref, b_ref, seqs, pick):
    parts = []
    for s in seqs:
        x, y, z = s // (NY * NZ), (s // NZ) % NY, s % NZ
        parts.append(a_ref[(y, x, z) + pick])
        parts.append(b_ref[(x, y, z) + pick])
    return jnp.concatenate(parts, axis=0)


def layer_kernel(
    length_ref, hidden_hbm, gain_hbm, shift_hbm, weight_hbm, bias_hbm, out_weight_hbm, out_bias_hbm,
    keys_hbm, values_hbm, table_hbm,
    out_ref, fresh_all,
    hid, norm, qa, qb, ka, kb, oa, ob, gain, shift, bias, out_bias, table, keys, values,
    kaug, vaug, kfresh, vfresh, queries, acc, tops, parts, sides, part_out, side_out, mine, att,
    load_sem, local_sem, move_sem, zsend, zrecv, send, recv, hsend, hrecv, gsend, grecv, psend, precv, tsend, trecv,
):
    p = Place()
    peers = [None, p.z_partner(), p.y_partner(), p.diagonal()]
    local = lax.rem(p.s, 4)
    target_seq = lax.rem(p.s, 8) * 8 + p.t
    target = (target_seq, lax.div(p.s, 8))
    source = (p.t * 8 + lax.div(p.s, 8), lax.rem(p.s, 8))
    away = target_seq != p.s
    away = jnp.logical_or(away, target[1] != p.t)
    steady = peers[1:] + [p.core_partner(), p.up(1), p.up(-1),
                          p.beside(0, 1), p.beside(0, -1), p.beside(1, 1), p.beside(1, -1)]
    barrier = pltpu.get_barrier_semaphore()
    for device in steady:
        pl.semaphore_signal(barrier, inc=1, device_id=device, device_id_type=MESH)

    @pl.when(away)
    def _():
        for device in (target, source):
            pl.semaphore_signal(barrier, inc=1, device_id=device, device_id_type=MESH)

    loads = {}
    for index, (name, src, dst) in enumerate((
        ("gain", gain_hbm, gain), ("shift", shift_hbm, shift), ("bias", bias_hbm, bias),
        ("out_bias", out_bias_hbm, out_bias), ("table", table_hbm.at[pl.ds(p.t * 2, 2)], table),
        ("keys", keys_hbm, keys), ("values", values_hbm, values),
    )):
        loads[name] = pltpu.make_async_copy(src, dst, load_sem.at[index])
        loads[name].start()

    pl.semaphore_wait(barrier, len(steady) + 2 * away.astype(jnp.int32))

    def gather(index, halves, bufs):
        return Gather(p, halves, bufs, local_sem.at[index], zsend.at[index], zrecv.at[index],
                      send.at[index], recv.at[index])

    lower, upper = pl.ds(0, 16), pl.ds(16, 16)
    q_gather = gather(0, [weight_hbm.at[0, lower], weight_hbm.at[0, upper]], (qa, qb))
    kv_gather = gather(1, [weight_hbm.at[pl.ds(1, 2), lower], weight_hbm.at[pl.ds(1, 2), upper]], (ka, kb))
    o_gather = gather(2, None, (oa, ob))
    tokens = TpGather(p, hidden_hbm, hid, local_sem.at[2, 0], hsend, hrecv)
    q_gather.begin()
    tokens.begin()

    tx, ty, tz = lax.div(target_seq, 16), lax.rem(lax.div(target_seq, 2), NY), lax.rem(target_seq, 2)
    places = [oa.at[ty, tx, tz], ob.at[tx, ty, tz]]
    pieces = [out_weight_hbm.at[lower], out_weight_hbm.at[upper]]
    moved = [remote(pieces[k], places[k], move_sem.at[k], move_sem.at[2 + k], target) for k in (0, 1)]
    stay = [pltpu.make_async_copy(pieces[k], places[k], move_sem.at[4 + k]) for k in (0, 1)]

    @pl.when(away)
    def _():
        for copy in moved:
            copy.start()

    @pl.when(jnp.logical_not(away))
    def _():
        for copy in stay:
            copy.start()

    kv_gather.begin()
    q_gather.roots()

    length = length_ref[lax.div(p.s, 4)]
    first = local * SLOTS - length

    def aux(count, start, cached):
        place = lax.broadcasted_iota(jnp.int32, (count, HEAD_DIM), 0) + start
        lane = lax.broadcasted_iota(jnp.int32, (count, HEAD_DIM), 1)
        high = lax.shift_right_arithmetic(place, 7)
        low = place - high * 128
        number = jnp.where(lane < 3, high, jnp.where(lane < 6, low, 0)).astype(F32)
        if cached:
            number = jnp.where(place >= 0, jnp.where(lane == 6, -1e30, 0.0), number)
        return number.astype(BF16)

    def ones(count):
        return jnp.where(lax.broadcasted_iota(jnp.int32, (count, HEAD_DIM), 1) == 0, 1.0, 0.0).astype(BF16)

    columns = [slice(0, HEAD_DIM), slice(HEAD_DIM, 2 * HEAD_DIM)]

    def prepare_keys():
        loads["keys"].wait()
        number = aux(SLOTS, first, True)
        alive = lax.broadcasted_iota(jnp.int32, (SLOTS, HEAD_DIM), 0) + first < 0
        for head in range(2):
            kaug[head, :, :HEAD_DIM] = jnp.where(alive, keys[:, columns[head]].astype(F32), 0.0).astype(BF16)
            kaug[head, :, HEAD_DIM:] = number

    def prepare_values():
        loads["values"].wait()
        for head in range(2):
            vaug[head, :, :HEAD_DIM] = values[:, columns[head]]
            vaug[head, :, HEAD_DIM:] = ones(SLOTS)

    def normalise(start, rows):
        numbers = [hid[t, start:start + rows, :].astype(F32) for t in range(TP)]
        mean = jnp.sum(functools.reduce(jnp.add, numbers), axis=1, keepdims=True) * (1.0 / (TP * ROWS))
        numbers = [v - mean for v in numbers]
        squares = functools.reduce(jnp.add, [v * v for v in numbers])
        variance = jnp.sum(squares, axis=1, keepdims=True) * (1.0 / (TP * ROWS))
        scale = lax.rsqrt(variance + 1e-05)
        for t in range(TP):
            cols = slice(t * ROWS, (t + 1) * ROWS)
            norm[t, start:start + rows, :] = (numbers[t] * scale * gain[:, cols] + shift[:, cols]).astype(BF16)

    def project(bufs, pick, row):
        total = None
        for t in range(TP):
            rows = weight_rows(bufs[0], bufs[1], range(t * 8, t * 8 + 8), pick)
            part = jnp.dot(norm[t], rows, preferred_element_type=F32)
            total = part if total is None else total + part
        return total + bias[row:row + 1, :]

    levels = [[n for n in ORDER if n.depth == d] for d in range(7)]

    def step(who, depth):
        for node in levels[depth]:
            who.take(node)

    prepare_keys()
    step(q_gather, 1)
    tokens.near()
    step(q_gather, 2)
    prepare_values()
    tokens.far()
    step(q_gather, 3)
    tokens.rest()
    kv_gather.roots()
    for name in ("gain", "shift", "bias", "out_bias", "table"):
        loads[name].wait()
    step(q_gather, 4)
    normalise(0, 128)
    step(q_gather, 5)
    normalise(128, 128)
    step(q_gather, 6)
    step(kv_gather, 1)
    queries[local] = (project((qa, qb), (), 0) * (LOG2E / math.sqrt(HEAD_DIM))).astype(BF16)
    sent = []

    def exchange(src, dst, sems, index, peer):
        copy = remote(src, dst, sems[0].at[index], sems[1].at[index], peer)
        copy.start()
        sent.append(copy)

    def arrived(dst, sems, index, peer):
        remote(dst, dst, sems[0].at[index], sems[1].at[index], peer).wait_recv()

    step(kv_gather, 2)
    for k in (1, 2, 3):
        exchange(queries.at[local], queries.at[local], (gsend, grecv), k, peers[k])

    def query_of(block, head):
        side = jnp.broadcast_to(table[head], (ROWS, HEAD_DIM)).astype(BF16)
        return jnp.concatenate([queries[block, :, columns[head]], side], axis=1)

    nt = (((1,), (1,)), ((), ()))

    def attend(k, block):
        for head in range(2):
            score = lax.dot_general(query_of(block, head), kaug[head], nt, preferred_element_type=F32)
            top = jnp.max(score, axis=1, keepdims=True)
            weight = jnp.exp2(score - top).astype(BF16)
            acc[2 * k + head] = jnp.dot(weight, vaug[head], preferred_element_type=F32)
            tops[2 * k + head] = jnp.broadcast_to(top, (ROWS, HEAD_DIM))

    blocks = [local] + [lax.rem(peer[0], 4) for peer in peers[1:]]
    attend(0, blocks[0])
    step(kv_gather, 3)
    arrived(queries.at[blocks[1]], (gsend, grecv), 1, peers[1])
    attend(1, blocks[1])
    step(kv_gather, 4)

    @pl.when(away)
    def _():
        for k in (0, 1):
            own = o_gather.own(k)
            remote(own, own, move_sem.at[k], move_sem.at[2 + k], source).wait_recv()
            moved[k].wait_send()

    @pl.when(jnp.logical_not(away))
    def _():
        for copy in stay:
            copy.wait()

    o_gather.begin()
    arrived(queries.at[blocks[2]], (gsend, grecv), 2, peers[2])
    attend(2, blocks[2])
    step(kv_gather, 5)
    arrived(queries.at[blocks[3]], (gsend, grecv), 3, peers[3])
    attend(3, blocks[3])
    step(kv_gather, 6)
    o_gather.roots()

    for which in range(2):
        fresh_all[local, which] = project((ka, kb), (which,), 1 + which).astype(BF16)
    number = aux(ROWS, local * ROWS, False)
    for head in range(2):
        kfresh[head, :, :HEAD_DIM] = fresh_all[local, 0, :, columns[head]]
        kfresh[head, :, HEAD_DIM:] = number
        vfresh[head, :, :HEAD_DIM] = fresh_all[local, 1, :, columns[head]]
        vfresh[head, :, HEAD_DIM:] = ones(ROWS)
    step(o_gather, 1)

    def attend_fresh(k, block, put_part, put_side):
        row = lax.broadcasted_iota(jnp.int32, (ROWS, ROWS), 0) + block * ROWS
        column = lax.broadcasted_iota(jnp.int32, (ROWS, ROWS), 1) + local * ROWS
        lses = []
        for head in range(2):
            score = lax.dot_general(query_of(block, head), kfresh[head], nt, preferred_element_type=F32)
            score = jnp.where(column <= row, score, -1e30)
            before = tops[2 * k + head][:, :1]
            top = jnp.maximum(before, jnp.max(score, axis=1, keepdims=True))
            weight = jnp.exp2(score - top).astype(BF16)
            both = jnp.dot(weight, vfresh[head], preferred_element_type=F32)
            both += acc[2 * k + head] * jnp.exp2(before - top)
            total = both[:, HEAD_DIM:HEAD_DIM + 1]
            put_part(columns[head], (both[:, :HEAD_DIM] / total).astype(BF16))
            lses.append(top + jnp.log2(total))
        lane = lax.broadcasted_iota(jnp.int32, (ROWS, HEAD_DIM), 1)
        put_side(jnp.transpose(jnp.where(lane == 0, lses[0], lses[1]))[:8])

    def put(ref, index):
        def store(cols, value):
            ref[index, :, cols] = value
        return store

    def put_all(ref, index):
        def store(value):
            ref[index] = value
        return store

    def send_part(k):
        exchange(part_out.at[k], parts.at[local], (psend, precv), k, peers[k])
        exchange(side_out.at[k], sides.at[local], (psend, precv), 4 + k, peers[k])

    attend_fresh(3, blocks[3], put(part_out, 3), put_all(side_out, 3))
    attend_fresh(2, blocks[2], put(part_out, 2), put_all(side_out, 2))
    send_part(3)
    attend_fresh(1, blocks[1], put(part_out, 1), put_all(side_out, 1))
    send_part(2)
    attend_fresh(0, blocks[0], put(parts, local), put_all(sides, local))
    send_part(1)
    exchange(fresh_all.at[local], fresh_all.at[local], (gsend, grecv), 4, peers[1])
    exchange(fresh_all.at[local], fresh_all.at[local], (gsend, grecv), 5, peers[2])
    step(o_gather, 2)
    for k in (3, 2, 1):
        arrived(parts.at[blocks[k]], (psend, precv), k, peers[k])
        arrived(sides.at[blocks[k]], (psend, precv), 4 + k, peers[k])
    stats = [sides[k] for k in range(4)]
    top = functools.reduce(jnp.maximum, stats)
    shares = [jnp.exp2(stat - top) for stat in stats]
    total = functools.reduce(jnp.add, shares)
    shares = [jnp.transpose(jnp.concatenate([share / total] * 16, axis=0)) for share in shares]
    for head in range(2):
        terms = [parts[k, :, columns[head]].astype(F32) * shares[k][:, head:head + 1] for k in range(4)]
        mine[:, columns[head]] = functools.reduce(jnp.add, terms).astype(BF16)
    tokens.finish()
    finals = TpGather(p, mine, att, local_sem.at[2, 1], tsend, trecv)
    finals.begin()
    step(o_gather, 3)
    finals.near()
    step(o_gather, 4)
    arrived(fresh_all.at[blocks[1]], (gsend, grecv), 4, peers[1])
    exchange(fresh_all.at[blocks[1]], fresh_all.at[blocks[1]], (gsend, grecv), 6, peers[2])
    finals.far()
    step(o_gather, 5)
    step(o_gather, 6)
    finals.rest()
    result = None
    for t in range(TP):
        rows = weight_rows(oa, ob, range(t, 64, TP), ())
        term = lax.dot_general(att[t], rows, nt, preferred_element_type=F32)
        result = term if result is None else result + term
    out_ref[...] = (result + out_bias[...]).astype(BF16)
    arrived(fresh_all.at[blocks[2]], (gsend, grecv), 5, peers[2])
    arrived(fresh_all.at[blocks[3]], (gsend, grecv), 6, peers[2])
    for copy in sent:
        copy.wait_send()
    for who in (q_gather, kv_gather, o_gather, finals):
        who.finish()


PAD = ROWS + 32


def cache_kernel(numbers_ref, all_ref, keys_ref, values_ref, keys_out, values_out, fresh):
    step = pl.program_id(0)

    @pl.when(step == 0)
    def _():
        for k in range(2):
            for h in range(2):
                fresh[2 * k + h, :PAD] = jnp.zeros((PAD, HEAD_DIM), F32)
                fresh[2 * k + h, PAD + SPAN:] = jnp.zeros((PAD, HEAD_DIM), F32)
                for block in range(4):
                    rows = all_ref[block, k, :, h * HEAD_DIM:(h + 1) * HEAD_DIM]
                    fresh[2 * k + h, PAD + block * ROWS:PAD + (block + 1) * ROWS] = rows.astype(F32)

    start = step * ROWS + numbers_ref[0]
    touched = (start > -ROWS) & (start < SPAN)

    @pl.when(touched)
    def _():
        begin = jnp.clip(start, -ROWS, SPAN)
        place = lax.broadcasted_iota(jnp.int32, (ROWS, HEAD_DIM), 0) + begin
        inside = (place >= 0) & (place < SPAN)
        for k, (old, new) in enumerate(((keys_ref, keys_out), (values_ref, values_out))):
            for h in range(2):
                cols = slice(h * HEAD_DIM, (h + 1) * HEAD_DIM)
                rows = fresh[2 * k + h, pl.ds(begin + PAD, ROWS), :]
                new[:, cols] = jnp.where(inside, rows, old[:, cols].astype(F32)).astype(BF16)

    @pl.when(jnp.logical_not(touched))
    def _():
        keys_out[...] = keys_ref[...]
        values_out[...] = values_ref[...]


def round_bf16(value):
    return np.asarray(np.asarray(value, np.float32).astype(jnp.bfloat16), np.float64)


def bias_table():
    table = np.zeros((HEADS, 1, HEAD_DIM), np.float64)
    for head in range(HEADS):
        slope = 2.0 ** (-8.0 * (head + 1) / HEADS) * LOG2E
        for column, value in ((0, slope * 128.0), (3, slope)):
            rest = value
            for k in range(3):
                table[head, 0, column + k] = round_bf16(rest)
                rest = rest - table[head, 0, column + k]
        table[head, 0, 6] = 1.0
    return table.astype(np.float32)


def dma(*count):
    return pltpu.SemaphoreType.DMA(count)


def on_device(
    hidden_in, norm_gain, norm_bias, qkv_weight, qkv_bias, out_weight, out_bias, key_cache, value_cache, cached_len,
):
    any_spec = pl.BlockSpec(memory_space=pl.ANY)

    def vm(*shape, dtype=BF16):
        return pltpu.VMEM(shape, dtype)

    mixed, shared = pl.pallas_call(
        layer_kernel,
        name="layer",
        out_shape=(
            jax.ShapeDtypeStruct((ROWS, ROWS), BF16),
            jax.ShapeDtypeStruct((4, 2, ROWS, ROWS), BF16),
        ),
        in_specs=[SMEM_SPEC] + [any_spec] * 10,
        out_specs=(VMEM_SPEC, VMEM_SPEC),
        scratch_shapes=[
            vm(TP, ROWS, ROWS), vm(TP, ROWS, ROWS),
            vm(NY, NX, NZ, 16, ROWS), vm(NX, NY, NZ, 16, ROWS),
            vm(NY, NX, NZ, 2, 16, ROWS), vm(NX, NY, NZ, 2, 16, ROWS),
            vm(NY, NX, NZ, 16, ROWS), vm(NX, NY, NZ, 16, ROWS),
            vm(1, TP * ROWS, dtype=F32), vm(1, TP * ROWS, dtype=F32), vm(3, ROWS, dtype=F32), vm(1, ROWS, dtype=F32),
            vm(2, 1, HEAD_DIM, dtype=F32), vm(SLOTS, ROWS), vm(SLOTS, ROWS),
            vm(2, SLOTS, ROWS), vm(2, SLOTS, ROWS), vm(2, ROWS, ROWS), vm(2, ROWS, ROWS),
            vm(4, ROWS, ROWS), vm(8, ROWS, ROWS, dtype=F32), vm(8, ROWS, HEAD_DIM, dtype=F32),
            vm(4, ROWS, ROWS), vm(4, 8, ROWS, dtype=F32), vm(4, ROWS, ROWS), vm(4, 8, ROWS, dtype=F32),
            vm(ROWS, ROWS), vm(TP, ROWS, ROWS),
            dma(7), dma(3, 2), dma(6), dma(3, 2), dma(3, 2), dma(3, N_EDGES), dma(3, N_EDGES),
            dma(8), dma(8), dma(7), dma(7), dma(8), dma(8), dma(8), dma(8),
        ],
        compiler_params=pltpu.CompilerParams(collective_id=0, has_side_effects=True, vmem_limit_bytes=56 << 20),
    )(
        cached_len, hidden_in, norm_gain.reshape(1, TP * ROWS), norm_bias.reshape(1, TP * ROWS),
        qkv_weight, qkv_bias, out_weight.T, out_bias.reshape(1, ROWS), key_cache, value_cache,
        jnp.asarray(bias_table()),
    )

    seq_index = lax.axis_index("seq")
    length = lax.dynamic_index_in_dim(cached_len, seq_index // 4, 0, keepdims=False)
    numbers = (seq_index % 4 * SLOTS - length).astype(jnp.int32).reshape(1)

    block = pl.BlockSpec((ROWS, ROWS), lambda j: (j, 0))
    keys_new, values_new = pl.pallas_call(
        cache_kernel,
        name="cache",
        grid=(SLOTS // ROWS,),
        out_shape=(jax.ShapeDtypeStruct((SLOTS, ROWS), BF16),) * 2,
        in_specs=[SMEM_SPEC, VMEM_SPEC, block, block],
        out_specs=(block, block),
        scratch_shapes=[pltpu.VMEM((4, SPAN + 2 * PAD, HEAD_DIM), F32)],
        compiler_params=pltpu.CompilerParams(vmem_limit_bytes=32 << 20),
    )(numbers, shared, key_cache, value_cache)
    return (mixed, keys_new, values_new)


def solution(mesh):
    placed = (
        P("seq", "tp"),
        P(),
        P(),
        P(None, "seq", "tp"),
        P(None, "tp"),
        P("tp", "seq"),
        P("tp"),
        P("seq", "tp"),
        P("seq", "tp"),
        P(),
    )
    return jax.shard_map(
        on_device,
        mesh=mesh,
        in_specs=placed,
        out_specs=(P("seq", "tp"), P("seq", "tp"), P("seq", "tp")),
        check_vma=False,
    )
```

time: 149 us -> 109 us (0.73)
  Pallas kernels: 133 us -> 103 us
  local copies, waits for them, and re-layouts: 8.92 us -> 3.13 us
  starting transfers between devices: 5.38 us -> 0 us
    pallas_call x4 -> x1, Pallas kernels: 128 us -> 99.5 us  [on_device(): pl.pallas_call(layer_kernel, name='layer', out_shape=(jax.ShapeDtypeStruc...]
    ppermute x1 -> x0, starting transfers between devices: 5.38 us -> none  [on_device(): out_block = lax.ppermute(out_weight.T, ('seq', 'tp'), moves)]
    unnamed x19 -> x9, local copies, waits for them, and re-layouts: 6.3 us -> 1.89 us
  transfers between devices with their start and end apart: 1 -> 0, of which waited for: 0 -> 0; matrix products, arithmetic and copies ran while one was open for 2% -> 0% of each run, Pallas kernels for 32% -> 0%
where the time goes in v2:
time: 109 us; the launch traced here: 108 us
  Pallas kernels  103 us (94%)
  local copies, waits for them, and re-layouts  3.13 us (3%)
  between operations  1.36 us (1%)
    pallas_call x1, Pallas kernels, on_device(): pl.pallas_call(layer_kernel, name='layer', out_shape=(jax.ShapeDtypeStruc...  99.5 us
    pallas_call x1, Pallas kernels, on_device(): pl.pallas_call(cache_kernel, name='cache', grid=(SLOTS // ROWS,), out_sha...  3.79 us

profile of v2, /device:TPU:1, one launch (start us, length us, event | category | flops | bytes accessed | tf_op | source)
XLA Modules:
  0.0 107.7 jit_solution(14431185053948746195)
XLA Ops:
  0.7 1.2 %dynamic_slice.4 = s32[1]{0:T(128)} dynamic-slice(s32[16]{0:T(128)} %length_ref.1, s32[]{:T(128)S(6)} %select_n.17), dynamic_slice_sizes={1} | dynamic-slice | bytes 12 | tf_op jit(solution)/shard_map/jit(dynamic_index_in_dim)/dynamic_slice | solution.py:626
  2.5 0.0 copy-start
  2.6 0.0 copy-start.1
  2.6 99.5 %layer.1 = (bf16[256,256]{1,0:T(8,128)(2,1)}, bf16[4,2,256,256]{3,2,1,0:T(8,128)(2,1)}) custom-call(s32[16]{0:T(128)} %length_ref.1, bf16[256,256]{1,0:T(8,128)(2,1)} %hidden_hbm.1, f32[1,2048]{1,0:T(1,128)} %bitcast.7, f32[1,2048]{1,0:T(1,128)} %bitcast.8, bf16[3,32,256]{2,1,0:T(8,128)(2,1)} %weight_hbm.1, f32[3,256]{1,0:T(4,128)} %bias_hbm.1, ...), custom_call_target="tpu_custom_call" | custom-call | tf_op jit(solution)/shard_map/layer/pallas_call | solution.py:595
  102.0 0.0 copy-done
  102.0 0.0 copy-done.1
  102.1 0.0 copy-start.2
  102.1 1.2 %copy-done.2 = bf16[4,2,256,256]{3,2,1,0:T(8,128)(2,1)S(1)} copy-done((bf16[4,2,256,256]{3,2,1,0:T(8,128)(2,1)S(1)}, bf16[4,2,256,256]{3,2,1,0:T(8,128)(2,1)}, u32[]{:S(2)}) %copy-start.2) | copy-done | bytes 1048600
  103.3 0.0 copy-start.3
  103.3 3.8 %cache.1 = (bf16[2304,256]{1,0:T(8,128)(2,1)}, bf16[2304,256]{1,0:T(8,128)(2,1)}) custom-call(s32[1]{0:T(128)} %bitcast.5.numbers_ref, bf16[4,2,256,256]{3,2,1,0:T(8,128)(2,1)S(1)} %copy-done.2, bf16[2304,256]{1,0:T(8,128)(2,1)S(1)} %copy-done, bf16[2304,256]{1,0:T(8,128)(2,1)S(1)} %copy-done.1), custom_call_target="tpu_custom_call" | custom-call | tf_op jit(solution)/shard_map/cache/pallas_call | solution.py:630
  107.1 0.0 copy-done.3
  107.1 0.7 copy.15
Async XLA Ops:
  2.5 99.5 %copy-start = (bf16[2304,256]{1,0:T(8,128)(2,1)S(1)}, bf16[2304,256]{1,0:T(8,128)(2,1)}, u32[]{:S(2)}) copy-start(bf16[2304,256]{1,0:T(8,128)(2,1)} %keys_ref.1) | copy-start | bytes 3538948
  2.6 99.5 %copy-start.1 = (bf16[2304,256]{1,0:T(8,128)(2,1)S(1)}, bf16[2304,256]{1,0:T(8,128)(2,1)}, u32[]{:S(2)}) copy-start(bf16[2304,256]{1,0:T(8,128)(2,1)} %values_ref.1) | copy-start | bytes 3538948
  102.1 1.2 %copy-start.2 = (bf16[4,2,256,256]{3,2,1,0:T(8,128)(2,1)S(1)}, bf16[4,2,256,256]{3,2,1,0:T(8,128)(2,1)}, u32[]{:S(2)}) copy-start(bf16[4,2,256,256]{3,2,1,0:T(8,128)(2,1)} %get-tuple-element.8.all_ref) | copy-start | bytes 3145732
  103.3 3.8 %copy-start.3 = (bf16[256,256]{1,0:T(8,128)(2,1)S(1)}, bf16[256,256]{1,0:T(8,128)(2,1)}, u32[]{:S(2)}) copy-start(bf16[256,256]{1,0:T(8,128)(2,1)} %get-tuple-element.14) | copy-start | bytes 393220

commit v3 on v2

--- a/solution.py
+++ b/solution.py
@@ -16,6 +16,7 @@
 NX, NY, NZ = 4, 8, 2
 TP = 8
 ROWS = 256
+PAD = ROWS + 32
 SLOTS = 2304
 LOG2E = 1.4426950408889634
 MESH = pl.DeviceIdType.MESH
@@ -34,39 +35,50 @@
         if parent is not None:
             parent.kids.append(self)
 
-
-def build_tree(tree):
-    root = Node(tree, 0, 0, None, None)
-
-    def ring(start, axis, far_up):
-        size = (NX, NY)[axis]
-        for sign in (1, -1):
-            most = size // 2 - (0 if (sign == 1) == far_up else 1)
-            node = start
-            for _ in range(most):
-                step = [0, 0]
-                step[axis] = -sign
-                node = Node(tree, node.ox + step[0], node.oy + step[1], (axis, sign), node)
-                yield node
-
-    first, second = (0, 1) if tree == 0 else (1, 0)
-    nodes = [root] + list(ring(root, first, True))
-    flip = {}
-    for node in list(nodes):
-        off = node.ox if first == 0 else node.oy
-        nodes += list(ring(node, second, (off % 2 == 0) if first == 1 else off in (0, -1)))
+    def grow(self, axis, hops):
+        return Node(self.tree, self.ox - hops * (axis == 0), self.oy - hops * (axis == 1), (axis, hops), self)
+
+
+def deep_ring(start, axis, far_up):
+    size = (NX, NY)[axis]
+    nodes = []
+    for sign in (1, -1):
+        node = start
+        for _ in range(size // 2 - (0 if (sign == 1) == far_up else 1)):
+            node = node.grow(axis, sign)
+            nodes.append(node)
     return nodes
 
 
-TREES = [build_tree(0), build_tree(1)]
-EDGES = []
-for _tree in TREES:
-    for _node in _tree:
-        if _node.parent is not None:
-            _node.sem = len(EDGES)
-            EDGES.append(_node)
-N_EDGES = len(EDGES)
-ORDER = sorted(EDGES, key=lambda n: (n.depth, n.sem))
+def shallow_ring(start, axis, far_up):
+    if axis == 0:
+        return [start.grow(0, 1), start.grow(0, -1), start.grow(0, 2 if far_up else -2)]
+    near = [start.grow(1, 1), start.grow(1, -1)]
+    far = [start.grow(1, 3), start.grow(1, -3)]
+    more = [near[0].grow(1, 1), near[1].grow(1, -1), far[0].grow(1, 1) if far_up else far[1].grow(1, -1)]
+    return near + far + more
+
+
+class Forest:
+    def __init__(self, ring):
+        self.roots, self.edges = [], []
+        for tree in (0, 1):
+            root = Node(tree, 0, 0, None, None)
+            nodes = [root] + ring(root, tree, True)
+            for node in list(nodes):
+                off = node.oy if tree else node.ox
+                nodes += ring(node, 1 - tree, off % 2 == 0 if tree else off in (0, -1))
+            self.roots.append(root)
+            self.edges += nodes[1:]
+        for index, node in enumerate(self.edges):
+            node.sem = index
+        self.depth = max(node.depth for node in self.edges)
+        order = sorted(self.edges, key=lambda n: (abs(n.way[1]), n.sem))
+        self.levels = [[n for n in order if n.depth == d] for d in range(self.depth + 1)]
+
+
+DEEP, SHALLOW = Forest(deep_ring), Forest(shallow_ring)
+N_EDGES = len(DEEP.edges)
 
 
 class Place:
@@ -118,8 +130,8 @@
 
 
 class Gather:
-    def __init__(self, place, halves, bufs, local_sem, zsend, zrecv, send, recv):
-        self.p, self.halves, self.bufs = place, halves, bufs
+    def __init__(self, place, forest, halves, bufs, local_sem, zsend, zrecv, send, recv):
+        self.p, self.forest, self.halves, self.bufs = place, forest, halves, bufs
         self.local_sem, self.zsend, self.zrecv, self.send, self.recv = local_sem, zsend, zrecv, send, recv
         self.sent = []
 
@@ -158,13 +170,17 @@
                 self.locals[k].wait()
             other = self.other(k)
             remote(other, other, self.zsend.at[k], self.zrecv.at[k], self.p.z_partner()).wait_recv()
-            self.forward(TREES[k][0])
+            self.forward(self.forest.roots[k])
 
     def take(self, node):
         piece = self.p.piece(self.bufs, node)
         way = (node.way[0], -node.way[1])
         remote(piece, piece, self.send.at[node.sem], self.recv.at[node.sem], self.p.beside(*way)).wait_recv()
         self.forward(node)
+
+    def step(self, depth):
+        for node in self.forest.levels[depth]:
+            self.take(node)
 
     def finish(self):
         for copy in self.sent:
@@ -241,8 +257,8 @@
 def layer_kernel(
     length_ref, hidden_hbm, gain_hbm, shift_hbm, weight_hbm, bias_hbm, out_weight_hbm, out_bias_hbm,
     keys_hbm, values_hbm, table_hbm,
-    out_ref, fresh_all,
-    hid, norm, qa, qb, ka, kb, oa, ob, gain, shift, bias, out_bias, table, keys, values,
+    out_ref, keys_out, values_out,
+    fresh_all, fresh, hid, norm, qa, qb, ra, rb, gain, shift, bias, out_bias, table, keys, values,
     kaug, vaug, kfresh, vfresh, queries, acc, tops, parts, sides, part_out, side_out, mine, att,
     load_sem, local_sem, move_sem, zsend, zrecv, send, recv, hsend, hrecv, gsend, grecv, psend, precv, tsend, trecv,
 ):
@@ -255,7 +271,8 @@
     away = target_seq != p.s
     away = jnp.logical_or(away, target[1] != p.t)
     steady = peers[1:] + [p.core_partner(), p.up(1), p.up(-1),
-                          p.beside(0, 1), p.beside(0, -1), p.beside(1, 1), p.beside(1, -1)]
+                          p.beside(0, 1), p.beside(0, -1), p.beside(0, 2),
+                          p.beside(1, 1), p.beside(1, -1), p.beside(1, 3), p.beside(1, -3)]
     barrier = pltpu.get_barrier_semaphore()
     for device in steady:
         pl.semaphore_signal(barrier, inc=1, device_id=device, device_id_type=MESH)
@@ -276,21 +293,20 @@
 
     pl.semaphore_wait(barrier, len(steady) + 2 * away.astype(jnp.int32))
 
-    def gather(index, halves, bufs):
-        return Gather(p, halves, bufs, local_sem.at[index], zsend.at[index], zrecv.at[index],
+    def gather(index, forest, halves, bufs):
+        return Gather(p, forest, halves, bufs, local_sem.at[index], zsend.at[index], zrecv.at[index],
                       send.at[index], recv.at[index])
 
     lower, upper = pl.ds(0, 16), pl.ds(16, 16)
-    q_gather = gather(0, [weight_hbm.at[0, lower], weight_hbm.at[0, upper]], (qa, qb))
-    kv_gather = gather(1, [weight_hbm.at[pl.ds(1, 2), lower], weight_hbm.at[pl.ds(1, 2), upper]], (ka, kb))
-    o_gather = gather(2, None, (oa, ob))
+    q_gather = gather(0, SHALLOW, [weight_hbm.at[0, lower], weight_hbm.at[0, upper]], (qa, qb))
+    rest = gather(1, DEEP, None, (ra, rb))
     tokens = TpGather(p, hidden_hbm, hid, local_sem.at[2, 0], hsend, hrecv)
     q_gather.begin()
     tokens.begin()
 
     tx, ty, tz = lax.div(target_seq, 16), lax.rem(lax.div(target_seq, 2), NY), lax.rem(target_seq, 2)
-    places = [oa.at[ty, tx, tz], ob.at[tx, ty, tz]]
     pieces = [out_weight_hbm.at[lower], out_weight_hbm.at[upper]]
+    places = [rb.at[tx, ty, tz, 2 + k] for k in (0, 1)]
     moved = [remote(pieces[k], places[k], move_sem.at[k], move_sem.at[2 + k], target) for k in (0, 1)]
     stay = [pltpu.make_async_copy(pieces[k], places[k], move_sem.at[4 + k]) for k in (0, 1)]
 
@@ -304,7 +320,12 @@
         for copy in stay:
             copy.start()
 
-    kv_gather.begin()
+    placed = [
+        pltpu.make_async_copy(weight_hbm.at[pl.ds(1, 2), rows], own.at[pl.ds(0, 2)], local_sem.at[1, k])
+        for k, (rows, own) in enumerate(((lower, rest.own(0)), (upper, rest.own(1))))
+    ]
+    for copy in placed:
+        copy.start()
     q_gather.roots()
 
     length = length_ref[lax.div(p.s, 4)]
@@ -321,7 +342,7 @@
         return number.astype(BF16)
 
     def ones(count):
-        return jnp.where(lax.broadcasted_iota(jnp.int32, (count, HEAD_DIM), 1) == 0, 1.0, 0.0).astype(BF16)
+        return jnp.ones((count, HEAD_DIM), BF16)
 
     columns = [slice(0, HEAD_DIM), slice(HEAD_DIM, 2 * HEAD_DIM)]
 
@@ -358,29 +379,36 @@
             total = part if total is None else total + part
         return total + bias[row:row + 1, :]
 
-    levels = [[n for n in ORDER if n.depth == d] for d in range(7)]
-
-    def step(who, depth):
-        for node in levels[depth]:
-            who.take(node)
-
     prepare_keys()
-    step(q_gather, 1)
+    q_gather.step(1)
     tokens.near()
-    step(q_gather, 2)
+
+    @pl.when(away)
+    def _():
+        for k in (0, 1):
+            own = rb.at[p.x, p.y, p.z, 2 + k]
+            remote(own, own, move_sem.at[k], move_sem.at[2 + k], source).wait_recv()
+            moved[k].wait_send()
+
+    @pl.when(jnp.logical_not(away))
+    def _():
+        for copy in stay:
+            copy.wait()
+
+    for copy in placed:
+        copy.wait()
+    rest.begin()
     prepare_values()
+    rest.roots()
+    q_gather.step(2)
     tokens.far()
-    step(q_gather, 3)
-    tokens.rest()
-    kv_gather.roots()
+    rest.step(1)
+    q_gather.step(3)
     for name in ("gain", "shift", "bias", "out_bias", "table"):
         loads[name].wait()
-    step(q_gather, 4)
+    tokens.rest()
     normalise(0, 128)
-    step(q_gather, 5)
     normalise(128, 128)
-    step(q_gather, 6)
-    step(kv_gather, 1)
     queries[local] = (project((qa, qb), (), 0) * (LOG2E / math.sqrt(HEAD_DIM))).astype(BF16)
     sent = []
 
@@ -392,7 +420,6 @@
     def arrived(dst, sems, index, peer):
         remote(dst, dst, sems[0].at[index], sems[1].at[index], peer).wait_recv()
 
-    step(kv_gather, 2)
     for k in (1, 2, 3):
         exchange(queries.at[local], queries.at[local], (gsend, grecv), k, peers[k])
 
@@ -412,41 +439,27 @@
 
     blocks = [local] + [lax.rem(peer[0], 4) for peer in peers[1:]]
     attend(0, blocks[0])
-    step(kv_gather, 3)
+    rest.step(2)
     arrived(queries.at[blocks[1]], (gsend, grecv), 1, peers[1])
     attend(1, blocks[1])
-    step(kv_gather, 4)
-
-    @pl.when(away)
-    def _():
-        for k in (0, 1):
-            own = o_gather.own(k)
-            remote(own, own, move_sem.at[k], move_sem.at[2 + k], source).wait_recv()
-            moved[k].wait_send()
-
-    @pl.when(jnp.logical_not(away))
-    def _():
-        for copy in stay:
-            copy.wait()
-
-    o_gather.begin()
+    rest.step(3)
     arrived(queries.at[blocks[2]], (gsend, grecv), 2, peers[2])
     attend(2, blocks[2])
-    step(kv_gather, 5)
+    rest.step(4)
     arrived(queries.at[blocks[3]], (gsend, grecv), 3, peers[3])
     attend(3, blocks[3])
-    step(kv_gather, 6)
-    o_gather.roots()
+    rest.step(5)
+    rest.step(6)
 
     for which in range(2):
-        fresh_all[local, which] = project((ka, kb), (which,), 1 + which).astype(BF16)
+        fresh_all[local, which] = project((ra, rb), (which,), 1 + which).astype(BF16)
+    exchange(fresh_all.at[local], fresh_all.at[local], (gsend, grecv), 4, peers[1])
     number = aux(ROWS, local * ROWS, False)
     for head in range(2):
         kfresh[head, :, :HEAD_DIM] = fresh_all[local, 0, :, columns[head]]
         kfresh[head, :, HEAD_DIM:] = number
         vfresh[head, :, :HEAD_DIM] = fresh_all[local, 1, :, columns[head]]
         vfresh[head, :, HEAD_DIM:] = ones(ROWS)
-    step(o_gather, 1)
 
     def attend_fresh(k, block, put_part, put_side):
         row = lax.broadcasted_iota(jnp.int32, (ROWS, ROWS), 0) + block * ROWS
@@ -455,13 +468,14 @@
         for head in range(2):
             score = lax.dot_general(query_of(block, head), kfresh[head], nt, preferred_element_type=F32)
             score = jnp.where(column <= row, score, -1e30)
-            before = tops[2 * k + head][:, :1]
+            before = tops[2 * k + head]
             top = jnp.maximum(before, jnp.max(score, axis=1, keepdims=True))
-            weight = jnp.exp2(score - top).astype(BF16)
+            weight = jnp.exp2(score - jnp.concatenate([top, top], axis=1)).astype(BF16)
+            keep = jnp.exp2(before - top)
             both = jnp.dot(weight, vfresh[head], preferred_element_type=F32)
-            both += acc[2 * k + head] * jnp.exp2(before - top)
-            total = both[:, HEAD_DIM:HEAD_DIM + 1]
-            put_part(columns[head], (both[:, :HEAD_DIM] / total).astype(BF16))
+            number = both[:, :HEAD_DIM] + acc[2 * k + head, :, :HEAD_DIM] * keep
+            total = both[:, HEAD_DIM:] + acc[2 * k + head, :, HEAD_DIM:] * keep
+            put_part(columns[head], (number / total).astype(BF16))
             lses.append(top + jnp.log2(total))
         lane = lax.broadcasted_iota(jnp.int32, (ROWS, HEAD_DIM), 1)
         put_side(jnp.transpose(jnp.where(lane == 0, lses[0], lses[1]))[:8])
@@ -487,9 +501,7 @@
     send_part(2)
     attend_fresh(0, blocks[0], put(parts, local), put_all(sides, local))
     send_part(1)
-    exchange(fresh_all.at[local], fresh_all.at[local], (gsend, grecv), 4, peers[1])
     exchange(fresh_all.at[local], fresh_all.at[local], (gsend, grecv), 5, peers[2])
-    step(o_gather, 2)
     for k in (3, 2, 1):
         arrived(parts.at[blocks[k]], (psend, precv), k, peers[k])
         arrived(sides.at[blocks[k]], (psend, precv), 4 + k, peers[k])
@@ -504,63 +516,72 @@
     tokens.finish()
     finals = TpGather(p, mine, att, local_sem.at[2, 1], tsend, trecv)
     finals.begin()
-    step(o_gather, 3)
-    finals.near()
-    step(o_gather, 4)
+    for k in range(2):
+        for h in range(2):
+            fresh[2 * k + h, :PAD] = jnp.zeros((PAD, HEAD_DIM), F32)
+            fresh[2 * k + h, PAD + SPAN:] = jnp.zeros((PAD, HEAD_DIM), F32)
     arrived(fresh_all.at[blocks[1]], (gsend, grecv), 4, peers[1])
     exchange(fresh_all.at[blocks[1]], fresh_all.at[blocks[1]], (gsend, grecv), 6, peers[2])
+    finals.near()
+    arrived(fresh_all.at[blocks[2]], (gsend, grecv), 5, peers[2])
     finals.far()
-    step(o_gather, 5)
-    step(o_gather, 6)
+    arrived(fresh_all.at[blocks[3]], (gsend, grecv), 6, peers[2])
+    stores = []
+    for k, (rows_of, out) in enumerate(((keys, keys_out), (values, values_out))):
+        for h in range(2):
+            for block in range(4):
+                begin = PAD + block * ROWS
+                fresh[2 * k + h, begin:begin + ROWS] = fresh_all[block, k, :, columns[h]].astype(F32)
+
+        for chunk in range(SLOTS // ROWS):
+            begin = jnp.clip(first + chunk * ROWS, -ROWS, SPAN)
+            place = lax.broadcasted_iota(jnp.int32, (ROWS, HEAD_DIM), 0) + begin
+            inside = (place >= 0) & (place < SPAN)
+            span = slice(chunk * ROWS, (chunk + 1) * ROWS)
+            for h in range(2):
+                new = fresh[2 * k + h, pl.ds(begin + PAD, ROWS), :]
+                old = rows_of[span, columns[h]].astype(F32)
+                rows_of[span, columns[h]] = jnp.where(inside, new, old).astype(BF16)
+        stores.append(pltpu.make_async_copy(rows_of, out, load_sem.at[7 + k]))
+        stores[-1].start()
     finals.rest()
+
+    def out_rows(seqs):
+        places = [(q // (NY * NZ), (q // NZ) % NY, q % NZ) for q in seqs]
+        return jnp.concatenate([rb[place + (2 + k,)] for place in places for k in (0, 1)], axis=0)
+
     result = None
     for t in range(TP):
-        rows = weight_rows(oa, ob, range(t, 64, TP), ())
+        rows = out_rows(range(t, 64, TP))
         term = lax.dot_general(att[t], rows, nt, preferred_element_type=F32)
         result = term if result is None else result + term
     out_ref[...] = (result + out_bias[...]).astype(BF16)
-    arrived(fresh_all.at[blocks[2]], (gsend, grecv), 5, peers[2])
-    arrived(fresh_all.at[blocks[3]], (gsend, grecv), 6, peers[2])
+    for copy in stores:
+        copy.wait()
     for copy in sent:
         copy.wait_send()
-    for who in (q_gather, kv_gather, o_gather, finals):
+    for who in (q_gather, rest, finals):
         who.finish()
 
 
-PAD = ROWS + 32
-
-
-def cache_kernel(numbers_ref, all_ref, keys_ref, values_ref, keys_out, values_out, fresh):
-    step = pl.program_id(0)
-
-    @pl.when(step == 0)
-    def _():
-        for k in range(2):
-            for h in range(2):
-                fresh[2 * k + h, :PAD] = jnp.zeros((PAD, HEAD_DIM), F32)
-                fresh[2 * k + h, PAD + SPAN:] = jnp.zeros((PAD, HEAD_DIM), F32)
-                for block in range(4):
-                    rows = all_ref[block, k, :, h * HEAD_DIM:(h + 1) * HEAD_DIM]
-                    fresh[2 * k + h, PAD + block * ROWS:PAD + (block + 1) * ROWS] = rows.astype(F32)
-
-    start = step * ROWS + numbers_ref[0]
-    touched = (start > -ROWS) & (start < SPAN)
-
-    @pl.when(touched)
-    def _():
-        begin = jnp.clip(start, -ROWS, SPAN)
-        place = lax.broadcasted_iota(jnp.int32, (ROWS, HEAD_DIM), 0) + begin
-        inside = (place >= 0) & (place < SPAN)
-        for k, (old, new) in enumerate(((keys_ref, keys_out), (values_ref, values_out))):
-            for h in range(2):
-                cols = slice(h * HEAD_DIM, (h + 1) * HEAD_DIM)
-                rows = fresh[2 * k + h, pl.ds(begin + PAD, ROWS), :]
-                new[:, cols] = jnp.where(inside, rows, old[:, cols].astype(F32)).astype(BF16)
-
-    @pl.when(jnp.logical_not(touched))
-    def _():
-        keys_out[...] = keys_ref[...]
-        values_out[...] = values_ref[...]
+def hand_over_kernel(mixed, keys, values, mixed_out, keys_out, values_out, a, b, c, in_sem, out_sem):
+    copies = []
+    for src, mid, dst, count in ((mixed, a, mixed_out, 1), (keys, b, keys_out, 4), (values, c, values_out, 4)):
+        rows = src.shape[0] // count
+        for k in range(count):
+            span = pl.ds(k * rows, rows)
+            index = len(copies)
+            copies.append((
+                pltpu.make_async_copy(src.at[span], mid.at[span], in_sem.at[index]),
+                pltpu.make_async_copy(mid.at[span], dst.at[span], out_sem.at[index]),
+            ))
+    for first, _ in copies:
+        first.start()
+    for first, second in copies:
+        first.wait()
+        second.start()
+    for _, second in copies:
+        second.wait()
 
 
 def round_bf16(value):
@@ -592,27 +613,28 @@
     def vm(*shape, dtype=BF16):
         return pltpu.VMEM(shape, dtype)
 
-    mixed, shared = pl.pallas_call(
+    results = pl.pallas_call(
         layer_kernel,
         name="layer",
         out_shape=(
             jax.ShapeDtypeStruct((ROWS, ROWS), BF16),
-            jax.ShapeDtypeStruct((4, 2, ROWS, ROWS), BF16),
+            jax.ShapeDtypeStruct((SLOTS, ROWS), BF16),
+            jax.ShapeDtypeStruct((SLOTS, ROWS), BF16),
         ),
         in_specs=[SMEM_SPEC] + [any_spec] * 10,
-        out_specs=(VMEM_SPEC, VMEM_SPEC),
+        out_specs=(VMEM_SPEC, any_spec, any_spec),
         scratch_shapes=[
+            vm(4, 2, ROWS, ROWS), vm(4, SPAN + 2 * PAD, HEAD_DIM, dtype=F32),
             vm(TP, ROWS, ROWS), vm(TP, ROWS, ROWS),
             vm(NY, NX, NZ, 16, ROWS), vm(NX, NY, NZ, 16, ROWS),
-            vm(NY, NX, NZ, 2, 16, ROWS), vm(NX, NY, NZ, 2, 16, ROWS),
-            vm(NY, NX, NZ, 16, ROWS), vm(NX, NY, NZ, 16, ROWS),
+            vm(NY, NX, NZ, 2, 16, ROWS), vm(NX, NY, NZ, 4, 16, ROWS),
             vm(1, TP * ROWS, dtype=F32), vm(1, TP * ROWS, dtype=F32), vm(3, ROWS, dtype=F32), vm(1, ROWS, dtype=F32),
             vm(2, 1, HEAD_DIM, dtype=F32), vm(SLOTS, ROWS), vm(SLOTS, ROWS),
             vm(2, SLOTS, ROWS), vm(2, SLOTS, ROWS), vm(2, ROWS, ROWS), vm(2, ROWS, ROWS),
             vm(4, ROWS, ROWS), vm(8, ROWS, ROWS, dtype=F32), vm(8, ROWS, HEAD_DIM, dtype=F32),
             vm(4, ROWS, ROWS), vm(4, 8, ROWS, dtype=F32), vm(4, ROWS, ROWS), vm(4, 8, ROWS, dtype=F32),
             vm(ROWS, ROWS), vm(TP, ROWS, ROWS),
-            dma(7), dma(3, 2), dma(6), dma(3, 2), dma(3, 2), dma(3, N_EDGES), dma(3, N_EDGES),
+            dma(9), dma(3, 2), dma(6), dma(2, 2), dma(2, 2), dma(2, N_EDGES), dma(2, N_EDGES),
             dma(8), dma(8), dma(7), dma(7), dma(8), dma(8), dma(8), dma(8),
         ],
         compiler_params=pltpu.CompilerParams(collective_id=0, has_side_effects=True, vmem_limit_bytes=56 << 20),
@@ -621,23 +643,14 @@
         qkv_weight, qkv_bias, out_weight.T, out_bias.reshape(1, ROWS), key_cache, value_cache,
         jnp.asarray(bias_table()),
     )
-
-    seq_index = lax.axis_index("seq")
-    length = lax.dynamic_index_in_dim(cached_len, seq_index // 4, 0, keepdims=False)
-    numbers = (seq_index % 4 * SLOTS - length).astype(jnp.int32).reshape(1)
-
-    block = pl.BlockSpec((ROWS, ROWS), lambda j: (j, 0))
-    keys_new, values_new = pl.pallas_call(
-        cache_kernel,
-        name="cache",
-        grid=(SLOTS // ROWS,),
-        out_shape=(jax.ShapeDtypeStruct((SLOTS, ROWS), BF16),) * 2,
-        in_specs=[SMEM_SPEC, VMEM_SPEC, block, block],
-        out_specs=(block, block),
-        scratch_shapes=[pltpu.VMEM((4, SPAN + 2 * PAD, HEAD_DIM), F32)],
-        compiler_params=pltpu.CompilerParams(vmem_limit_bytes=32 << 20),
-    )(numbers, shared, key_cache, value_cache)
-    return (mixed, keys_new, values_new)
+    return pl.pallas_call(
+        hand_over_kernel,
+        name="hand_over",
+        out_shape=tuple(jax.ShapeDtypeStruct(r.shape, r.dtype) for r in results),
+        in_specs=[any_spec] * 3,
+        out_specs=(any_spec,) * 3,
+        scratch_shapes=[vm(ROWS, ROWS), vm(SLOTS, ROWS), vm(SLOTS, ROWS), dma(9), dma(9)],
+    )(*results)
 
 
 def solution(mesh):

time: 109 us -> 97.7 us (0.90)
  Pallas kernels: 103 us -> 96.7 us
  local copies, waits for them, and re-layouts: 3.13 us -> 0 us
    pallas_call x1, Pallas kernels: 99.5 us -> 94.1 us  [on_device(): pl.pallas_call(layer_kernel, name='layer', out_shape=(jax.ShapeDtypeStruc...]
    unnamed x9 -> x0, local copies, waits for them, and re-layouts: 1.89 us -> none
    dynamic_slice x1 -> x0, local copies, waits for them, and re-layouts: 1.24 us -> none  [on_device(): lax.dynamic_index_in_dim(cached_len, seq_index // 4, 0, keepdims=False)]
    pallas_call x1, Pallas kernels: 3.79 us -> 2.58 us  [on_device(): pl.pallas_call(hand_over_kernel, name='hand_over', out_shape=tuple((jax.S...]
where the time goes in v3:
time: 97.7 us; the launch traced here: 97.5 us
  Pallas kernels  96.7 us (99%)
    pallas_call x1, Pallas kernels, on_device(): pl.pallas_call(layer_kernel, name='layer', out_shape=(jax.ShapeDtypeStruc...  94.1 us
    pallas_call x1, Pallas kernels, on_device(): pl.pallas_call(hand_over_kernel, name='hand_over', out_shape=tuple((jax.S...  2.58 us

profile of v3, /device:TPU:1, one launch (start us, length us, event | category | flops | bytes accessed | tf_op | source)
XLA Modules:
  0.0 97.5 jit_solution(17583262140731516745)
XLA Ops:
  0.6 94.1 %layer.1 = (bf16[256,256]{1,0:T(8,128)(2,1)}, bf16[2304,256]{1,0:T(8,128)(2,1)}, bf16[2304,256]{1,0:T(8,128)(2,1)}) custom-call(s32[16]{0:T(128)} %length_ref.1, bf16[256,256]{1,0:T(8,128)(2,1)} %hidden_hbm.1, f32[1,2048]{1,0:T(1,128)} %bitcast.5, f32[1,2048]{1,0:T(1,128)} %bitcast.6, bf16[3,32,256]{2,1,0:T(8,128)(2,1)} %weight_hbm.1, f32[3,256]{1,0:T(4,128)} %bias_hbm.1, ...), custom_call_target="tpu_custom_call" | custom-call | tf_op jit(solution)/shard_map/layer/pallas_call | solution.py:616
  94.8 2.6 %hand_over.1 = (bf16[256,256]{1,0:T(8,128)(2,1)}, bf16[2304,256]{1,0:T(8,128)(2,1)}, bf16[2304,256]{1,0:T(8,128)(2,1)}) custom-call(bf16[256,256]{1,0:T(8,128)(2,1)} %get-tuple-element.6.mixed, bf16[2304,256]{1,0:T(8,128)(2,1)} %get-tuple-element.7.keys, bf16[2304,256]{1,0:T(8,128)(2,1)} %get-tuple-element.8.values), custom_call_target="tpu_custom_call" | custom-call | tf_op jit(solution)/shard_map/hand_over/pallas_call | solution.py:646

commit v4 on v3

--- a/solution.py
+++ b/solution.py
@@ -60,15 +60,15 @@
 
 
 class Forest:
-    def __init__(self, ring):
-        self.roots, self.edges = [], []
-        for tree in (0, 1):
+    def __init__(self, ring, trees):
+        self.trees, self.roots, self.edges = trees, {}, []
+        for tree in trees:
             root = Node(tree, 0, 0, None, None)
             nodes = [root] + ring(root, tree, True)
             for node in list(nodes):
                 off = node.oy if tree else node.ox
                 nodes += ring(node, 1 - tree, off % 2 == 0 if tree else off in (0, -1))
-            self.roots.append(root)
+            self.roots[tree] = root
             self.edges += nodes[1:]
         for index, node in enumerate(self.edges):
             node.sem = index
@@ -77,7 +77,7 @@
         self.levels = [[n for n in order if n.depth == d] for d in range(self.depth + 1)]
 
 
-DEEP, SHALLOW = Forest(deep_ring), Forest(shallow_ring)
+DEEP, SHALLOW, LAST = Forest(deep_ring, (0, 1)), Forest(shallow_ring, (0, 1)), Forest(shallow_ring, (1,))
 N_EDGES = len(DEEP.edges)
 
 
@@ -145,14 +145,14 @@
 
     def begin(self):
         self.locals = []
-        for k in (0, 1):
+        for k in self.forest.trees:
             src = self.own(k) if self.halves is None else self.halves[k]
             copy = remote(src, self.own(k), self.zsend.at[k], self.zrecv.at[k], self.p.z_partner())
             copy.start()
             self.sent.append(copy)
         if self.halves is None:
             return
-        for k in (0, 1):
+        for k in self.forest.trees:
             copy = pltpu.make_async_copy(self.halves[k], self.own(k), self.local_sem.at[k])
             copy.start()
             self.locals.append(copy)
@@ -165,7 +165,7 @@
             self.sent.append(copy)
 
     def roots(self):
-        for k in (0, 1):
+        for k in self.forest.trees:
             if self.locals:
                 self.locals[k].wait()
             other = self.other(k)
@@ -208,21 +208,29 @@
 
     def begin(self):
         p = self.p
-        self.start(self.src, self.block(0), 0, p.up(1))
-        self.start(self.src, self.block(0), 1, p.up(-1))
-        self.start(self.src, self.block(0), 4, p.core_partner())
-        self.local = pltpu.make_async_copy(self.src, self.block(0), self.local_sem)
+        half = ROWS // 2
+        lower, upper = pl.ds(0, half), pl.ds(half, half)
+        mine = self.block(0)
+        self.start(self.src.at[lower], mine.at[lower], 0, p.up(1))
+        self.start(self.src.at[upper], mine.at[upper], 1, p.up(-1))
+        self.start(self.src.at[upper], mine.at[upper], 8, p.up(1))
+        self.start(self.src.at[lower], mine.at[lower], 9, p.up(-1))
+        self.start(self.src, mine, 4, p.core_partner())
+        self.local = pltpu.make_async_copy(self.src, mine, self.local_sem)
         self.local.start()
 
     def near(self):
         p = self.p
         half = ROWS // 2
+        lower, upper = pl.ds(0, half), pl.ds(half, half)
         low, high = self.block(-1), self.block(1)
-        self.copy(low, low, 0, p.up(-1)).wait_recv()
-        self.start(low.at[pl.ds(0, half)], low.at[pl.ds(0, half)], 2, p.up(1))
+        self.copy(low.at[lower], low.at[lower], 0, p.up(-1)).wait_recv()
+        self.start(low.at[lower], low.at[lower], 2, p.up(1))
+        self.copy(high.at[upper], high.at[upper], 1, p.up(1)).wait_recv()
+        self.start(high.at[upper], high.at[upper], 3, p.up(-1))
+        self.copy(low.at[upper], low.at[upper], 8, p.up(-1)).wait_recv()
         self.start(low, low, 5, p.core_partner())
-        self.copy(high, high, 1, p.up(1)).wait_recv()
-        self.start(high.at[pl.ds(half, half)], high.at[pl.ds(half, half)], 3, p.up(-1))
+        self.copy(high.at[lower], high.at[lower], 9, p.up(1)).wait_recv()
         self.start(high, high, 6, p.core_partner())
 
     def far(self):
@@ -245,20 +253,11 @@
             copy.wait_send()
 
 
-def weight_rows(a_ref, b_ref, seqs, pick):
-    parts = []
-    for s in seqs:
-        x, y, z = s // (NY * NZ), (s // NZ) % NY, s % NZ
-        parts.append(a_ref[(y, x, z) + pick])
-        parts.append(b_ref[(x, y, z) + pick])
-    return jnp.concatenate(parts, axis=0)
-
-
 def layer_kernel(
     length_ref, hidden_hbm, gain_hbm, shift_hbm, weight_hbm, bias_hbm, out_weight_hbm, out_bias_hbm,
     keys_hbm, values_hbm, table_hbm,
     out_ref, keys_out, values_out,
-    fresh_all, fresh, hid, norm, qa, qb, ra, rb, gain, shift, bias, out_bias, table, keys, values,
+    fresh_all, fresh, hid, norm, qa, qb, ka, kb, ob, gain, shift, bias, out_bias, table, keys, values,
     kaug, vaug, kfresh, vfresh, queries, acc, tops, parts, sides, part_out, side_out, mine, att,
     load_sem, local_sem, move_sem, zsend, zrecv, send, recv, hsend, hrecv, gsend, grecv, psend, precv, tsend, trecv,
 ):
@@ -299,14 +298,27 @@
 
     lower, upper = pl.ds(0, 16), pl.ds(16, 16)
     q_gather = gather(0, SHALLOW, [weight_hbm.at[0, lower], weight_hbm.at[0, upper]], (qa, qb))
-    rest = gather(1, DEEP, None, (ra, rb))
+    kv_gather = gather(1, DEEP, None, (ka, kb))
+    o_gather = gather(2, LAST, None, (None, ob))
     tokens = TpGather(p, hidden_hbm, hid, local_sem.at[2, 0], hsend, hrecv)
+    placed = [
+        pltpu.make_async_copy(weight_hbm.at[index, rows], place, local_sem.at[1, k])
+        for k, (index, rows, place) in enumerate((
+            (1, lower, kv_gather.own(0).at[0]), (1, upper, kv_gather.own(1).at[0]),
+            (2, lower, kv_gather.own(1).at[1]), (2, upper, kv_gather.own(1).at[2]),
+        ))
+    ]
+    for copy in placed:
+        copy.start()
     q_gather.begin()
     tokens.begin()
+    for copy in placed:
+        copy.wait()
+    kv_gather.begin()
 
     tx, ty, tz = lax.div(target_seq, 16), lax.rem(lax.div(target_seq, 2), NY), lax.rem(target_seq, 2)
     pieces = [out_weight_hbm.at[lower], out_weight_hbm.at[upper]]
-    places = [rb.at[tx, ty, tz, 2 + k] for k in (0, 1)]
+    places = [ob.at[tx, ty, tz, k] for k in (0, 1)]
     moved = [remote(pieces[k], places[k], move_sem.at[k], move_sem.at[2 + k], target) for k in (0, 1)]
     stay = [pltpu.make_async_copy(pieces[k], places[k], move_sem.at[4 + k]) for k in (0, 1)]
 
@@ -320,13 +332,8 @@
         for copy in stay:
             copy.start()
 
-    placed = [
-        pltpu.make_async_copy(weight_hbm.at[pl.ds(1, 2), rows], own.at[pl.ds(0, 2)], local_sem.at[1, k])
-        for k, (rows, own) in enumerate(((lower, rest.own(0)), (upper, rest.own(1))))
-    ]
-    for copy in placed:
-        copy.start()
     q_gather.roots()
+    kv_gather.roots()
 
     length = length_ref[lax.div(p.s, 4)]
     first = local * SLOTS - length
@@ -371,10 +378,25 @@
             cols = slice(t * ROWS, (t + 1) * ROWS)
             norm[t, start:start + rows, :] = (numbers[t] * scale * gain[:, cols] + shift[:, cols]).astype(BF16)
 
-    def project(bufs, pick, row):
+    def places(seqs):
+        return [(q // (NY * NZ), (q // NZ) % NY, q % NZ) for q in seqs]
+
+    def q_rows(seqs):
+        return [ref for x, y, z in places(seqs) for ref in (qa[y, x, z], qb[x, y, z])]
+
+    def k_rows(seqs):
+        return [ref for x, y, z in places(seqs) for ref in (ka[y, x, z, 0], kb[x, y, z, 0])]
+
+    def v_rows(seqs):
+        return [ref for x, y, z in places(seqs) for ref in (kb[x, y, z, 1], kb[x, y, z, 2])]
+
+    def out_rows(seqs):
+        return [ref for x, y, z in places(seqs) for ref in (ob[x, y, z, 0], ob[x, y, z, 1])]
+
+    def project(rows_of, row):
         total = None
         for t in range(TP):
-            rows = weight_rows(bufs[0], bufs[1], range(t * 8, t * 8 + 8), pick)
+            rows = jnp.concatenate(rows_of(range(t * 8, t * 8 + 8)), axis=0)
             part = jnp.dot(norm[t], rows, preferred_element_type=F32)
             total = part if total is None else total + part
         return total + bias[row:row + 1, :]
@@ -382,11 +404,17 @@
     prepare_keys()
     q_gather.step(1)
     tokens.near()
+    kv_gather.step(1)
+    prepare_values()
+    q_gather.step(2)
+    tokens.far()
+    kv_gather.step(2)
+    q_gather.step(3)
 
     @pl.when(away)
     def _():
         for k in (0, 1):
-            own = rb.at[p.x, p.y, p.z, 2 + k]
+            own = ob.at[p.x, p.y, p.z, k]
             remote(own, own, move_sem.at[k], move_sem.at[2 + k], source).wait_recv()
             moved[k].wait_send()
 
@@ -395,21 +423,13 @@
         for copy in stay:
             copy.wait()
 
-    for copy in placed:
-        copy.wait()
-    rest.begin()
-    prepare_values()
-    rest.roots()
-    q_gather.step(2)
-    tokens.far()
-    rest.step(1)
-    q_gather.step(3)
+    o_gather.begin()
     for name in ("gain", "shift", "bias", "out_bias", "table"):
         loads[name].wait()
     tokens.rest()
     normalise(0, 128)
     normalise(128, 128)
-    queries[local] = (project((qa, qb), (), 0) * (LOG2E / math.sqrt(HEAD_DIM))).astype(BF16)
+    queries[local] = (project(q_rows, 0) * (LOG2E / math.sqrt(HEAD_DIM))).astype(BF16)
     sent = []
 
     def exchange(src, dst, sems, index, peer):
@@ -438,22 +458,21 @@
             tops[2 * k + head] = jnp.broadcast_to(top, (ROWS, HEAD_DIM))
 
     blocks = [local] + [lax.rem(peer[0], 4) for peer in peers[1:]]
+    kv_gather.step(3)
     attend(0, blocks[0])
-    rest.step(2)
+    kv_gather.step(4)
     arrived(queries.at[blocks[1]], (gsend, grecv), 1, peers[1])
     attend(1, blocks[1])
-    rest.step(3)
+    kv_gather.step(5)
     arrived(queries.at[blocks[2]], (gsend, grecv), 2, peers[2])
     attend(2, blocks[2])
-    rest.step(4)
-    arrived(queries.at[blocks[3]], (gsend, grecv), 3, peers[3])
-    attend(3, blocks[3])
-    rest.step(5)
-    rest.step(6)
-
-    for which in range(2):
-        fresh_all[local, which] = project((ra, rb), (which,), 1 + which).astype(BF16)
-    exchange(fresh_all.at[local], fresh_all.at[local], (gsend, grecv), 4, peers[1])
+    kv_gather.step(6)
+    o_gather.roots()
+    for which, rows_of in ((0, k_rows), (1, v_rows)):
+        fresh_all[local, which] = project(rows_of, 1 + which).astype(BF16)
+        if which == 0:
+            exchange(fresh_all.at[local, 0], fresh_all.at[local, 0], (gsend, grecv), 4, peers[1])
+            exchange(fresh_all.at[local, 0], fresh_all.at[local, 0], (gsend, grecv), 5, peers[2])
     number = aux(ROWS, local * ROWS, False)
     for head in range(2):
         kfresh[head, :, :HEAD_DIM] = fresh_all[local, 0, :, columns[head]]
@@ -494,15 +513,22 @@
         exchange(part_out.at[k], parts.at[local], (psend, precv), k, peers[k])
         exchange(side_out.at[k], sides.at[local], (psend, precv), 4 + k, peers[k])
 
+    attend_fresh(1, blocks[1], put(part_out, 1), put_all(side_out, 1))
+    attend_fresh(2, blocks[2], put(part_out, 2), put_all(side_out, 2))
+    send_part(1)
+    arrived(queries.at[blocks[3]], (gsend, grecv), 3, peers[3])
+    send_part(2)
+    attend(3, blocks[3])
     attend_fresh(3, blocks[3], put(part_out, 3), put_all(side_out, 3))
-    attend_fresh(2, blocks[2], put(part_out, 2), put_all(side_out, 2))
+    attend_fresh(0, blocks[0], put(parts, local), put_all(sides, local))
     send_part(3)
-    attend_fresh(1, blocks[1], put(part_out, 1), put_all(side_out, 1))
-    send_part(2)
-    attend_fresh(0, blocks[0], put(parts, local), put_all(sides, local))
-    send_part(1)
-    exchange(fresh_all.at[local], fresh_all.at[local], (gsend, grecv), 5, peers[2])
-    for k in (3, 2, 1):
+    exchange(fresh_all.at[local, 1], fresh_all.at[local, 1], (gsend, grecv), 6, peers[1])
+    exchange(fresh_all.at[local, 1], fresh_all.at[local, 1], (gsend, grecv), 7, peers[2])
+    key_block = fresh_all.at[blocks[1], 0]
+    arrived(key_block, (gsend, grecv), 4, peers[1])
+    exchange(key_block, key_block, (gsend, grecv), 8, peers[2])
+    o_gather.step(1)
+    for k in (1, 2, 3):
         arrived(parts.at[blocks[k]], (psend, precv), k, peers[k])
         arrived(sides.at[blocks[k]], (psend, precv), 4 + k, peers[k])
     stats = [sides[k] for k in range(4)]
@@ -520,12 +546,16 @@
         for h in range(2):
             fresh[2 * k + h, :PAD] = jnp.zeros((PAD, HEAD_DIM), F32)
             fresh[2 * k + h, PAD + SPAN:] = jnp.zeros((PAD, HEAD_DIM), F32)
-    arrived(fresh_all.at[blocks[1]], (gsend, grecv), 4, peers[1])
-    exchange(fresh_all.at[blocks[1]], fresh_all.at[blocks[1]], (gsend, grecv), 6, peers[2])
     finals.near()
-    arrived(fresh_all.at[blocks[2]], (gsend, grecv), 5, peers[2])
+    o_gather.step(2)
+    value_block = fresh_all.at[blocks[1], 1]
+    arrived(value_block, (gsend, grecv), 6, peers[1])
+    exchange(value_block, value_block, (gsend, grecv), 9, peers[2])
     finals.far()
-    arrived(fresh_all.at[blocks[3]], (gsend, grecv), 6, peers[2])
+    arrived(fresh_all.at[blocks[2], 0], (gsend, grecv), 5, peers[2])
+    arrived(fresh_all.at[blocks[2], 1], (gsend, grecv), 7, peers[2])
+    arrived(fresh_all.at[blocks[3], 0], (gsend, grecv), 8, peers[2])
+    arrived(fresh_all.at[blocks[3], 1], (gsend, grecv), 9, peers[2])
     stores = []
     for k, (rows_of, out) in enumerate(((keys, keys_out), (values, values_out))):
         for h in range(2):
@@ -544,15 +574,12 @@
                 rows_of[span, columns[h]] = jnp.where(inside, new, old).astype(BF16)
         stores.append(pltpu.make_async_copy(rows_of, out, load_sem.at[7 + k]))
         stores[-1].start()
+    o_gather.step(3)
     finals.rest()
-
-    def out_rows(seqs):
-        places = [(q // (NY * NZ), (q // NZ) % NY, q % NZ) for q in seqs]
-        return jnp.concatenate([rb[place + (2 + k,)] for place in places for k in (0, 1)], axis=0)
 
     result = None
     for t in range(TP):
-        rows = out_rows(range(t, 64, TP))
+        rows = jnp.concatenate(out_rows(range(t, 64, TP)), axis=0)
         term = lax.dot_general(att[t], rows, nt, preferred_element_type=F32)
         result = term if result is None else result + term
     out_ref[...] = (result + out_bias[...]).astype(BF16)
@@ -560,7 +587,7 @@
         copy.wait()
     for copy in sent:
         copy.wait_send()
-    for who in (q_gather, rest, finals):
+    for who in (q_gather, kv_gather, o_gather, finals):
         who.finish()
 
 
@@ -627,15 +654,15 @@
             vm(4, 2, ROWS, ROWS), vm(4, SPAN + 2 * PAD, HEAD_DIM, dtype=F32),
             vm(TP, ROWS, ROWS), vm(TP, ROWS, ROWS),
             vm(NY, NX, NZ, 16, ROWS), vm(NX, NY, NZ, 16, ROWS),
-            vm(NY, NX, NZ, 2, 16, ROWS), vm(NX, NY, NZ, 4, 16, ROWS),
+            vm(NY, NX, NZ, 1, 16, ROWS), vm(NX, NY, NZ, 3, 16, ROWS), vm(NX, NY, NZ, 2, 16, ROWS),
             vm(1, TP * ROWS, dtype=F32), vm(1, TP * ROWS, dtype=F32), vm(3, ROWS, dtype=F32), vm(1, ROWS, dtype=F32),
             vm(2, 1, HEAD_DIM, dtype=F32), vm(SLOTS, ROWS), vm(SLOTS, ROWS),
             vm(2, SLOTS, ROWS), vm(2, SLOTS, ROWS), vm(2, ROWS, ROWS), vm(2, ROWS, ROWS),
             vm(4, ROWS, ROWS), vm(8, ROWS, ROWS, dtype=F32), vm(8, ROWS, HEAD_DIM, dtype=F32),
             vm(4, ROWS, ROWS), vm(4, 8, ROWS, dtype=F32), vm(4, ROWS, ROWS), vm(4, 8, ROWS, dtype=F32),
             vm(ROWS, ROWS), vm(TP, ROWS, ROWS),
-            dma(9), dma(3, 2), dma(6), dma(2, 2), dma(2, 2), dma(2, N_EDGES), dma(2, N_EDGES),
-            dma(8), dma(8), dma(7), dma(7), dma(8), dma(8), dma(8), dma(8),
+            dma(9), dma(3, 4), dma(6), dma(3, 2), dma(3, 2), dma(3, N_EDGES), dma(3, N_EDGES),
+            dma(10), dma(10), dma(10), dma(10), dma(8), dma(8), dma(10), dma(10),
         ],
         compiler_params=pltpu.CompilerParams(collective_id=0, has_side_effects=True, vmem_limit_bytes=56 << 20),
     )(

time: 97.7 us -> 90.1 us (0.922)
  Pallas kernels: 96.7 us -> 89.1 us
    pallas_call x1, Pallas kernels: 94.1 us -> 86.5 us  [on_device(): pl.pallas_call(layer_kernel, name='layer', out_shape=(jax.ShapeDtypeStruc...]
where the time goes in v4:
time: 90.1 us; the launch traced here: 89.9 us
  Pallas kernels  89.1 us (99%)
    pallas_call x1, Pallas kernels, on_device(): pl.pallas_call(layer_kernel, name='layer', out_shape=(jax.ShapeDtypeStruc...  86.5 us
    pallas_call x1, Pallas kernels, on_device(): pl.pallas_call(hand_over_kernel, name='hand_over', out_shape=tuple((jax.S...  2.58 us

profile of v4, /device:TPU:1, one launch (start us, length us, event | category | flops | bytes accessed | tf_op | source)
XLA Modules:
  0.0 89.9 jit_solution(12856067608636140952)
XLA Ops:
  0.6 86.5 %layer.1 = (bf16[256,256]{1,0:T(8,128)(2,1)}, bf16[2304,256]{1,0:T(8,128)(2,1)}, bf16[2304,256]{1,0:T(8,128)(2,1)}) custom-call(s32[16]{0:T(128)} %length_ref.1, bf16[256,256]{1,0:T(8,128)(2,1)} %hidden_hbm.1, f32[1,2048]{1,0:T(1,128)} %bitcast.5, f32[1,2048]{1,0:T(1,128)} %bitcast.6, bf16[3,32,256]{2,1,0:T(8,128)(2,1)} %weight_hbm.1, f32[3,256]{1,0:T(4,128)} %bias_hbm.1, ...), custom_call_target="tpu_custom_call" | custom-call | tf_op jit(solution)/shard_map/layer/pallas_call | solution.py:643
  87.1 2.6 %hand_over.1 = (bf16[256,256]{1,0:T(8,128)(2,1)}, bf16[2304,256]{1,0:T(8,128)(2,1)}, bf16[2304,256]{1,0:T(8,128)(2,1)}) custom-call(bf16[256,256]{1,0:T(8,128)(2,1)} %get-tuple-element.6.mixed, bf16[2304,256]{1,0:T(8,128)(2,1)} %get-tuple-element.7.keys, bf16[2304,256]{1,0:T(8,128)(2,1)} %get-tuple-element.8.values), custom_call_target="tpu_custom_call" | custom-call | tf_op jit(solution)/shard_map/hand_over/pallas_call | solution.py:673

commit v5 on v4

--- a/solution.py
+++ b/solution.py
@@ -311,10 +311,10 @@
     for copy in placed:
         copy.start()
     q_gather.begin()
-    tokens.begin()
     for copy in placed:
         copy.wait()
     kv_gather.begin()
+    tokens.begin()
 
     tx, ty, tz = lax.div(target_seq, 16), lax.rem(lax.div(target_seq, 2), NY), lax.rem(target_seq, 2)
     pieces = [out_weight_hbm.at[lower], out_weight_hbm.at[upper]]
@@ -333,7 +333,6 @@
             copy.start()
 
     q_gather.roots()
-    kv_gather.roots()
 
     length = length_ref[lax.div(p.s, 4)]
     first = local * SLOTS - length
@@ -402,6 +401,7 @@
         return total + bias[row:row + 1, :]
 
     prepare_keys()
+    kv_gather.roots()
     q_gather.step(1)
     tokens.near()
     kv_gather.step(1)

time: 90.1 us -> 91.1 us (1.011); the launches traced: 89.9 us -> 89.3 us
  no operation moved by 1% of the time
where the time goes in v5:
time: 91.1 us; the launch traced here: 89.3 us
  Pallas kernels  88.5 us (97%)
    pallas_call x1, Pallas kernels, on_device(): pl.pallas_call(layer_kernel, name='layer', out_shape=(jax.ShapeDtypeStruc...  86 us
    pallas_call x1, Pallas kernels, on_device(): pl.pallas_call(hand_over_kernel, name='hand_over', out_shape=tuple((jax.S...  2.58 us

profile of v5, /device:TPU:1, one launch (start us, length us, event | category | flops | bytes accessed | tf_op | source)
XLA Modules:
  0.0 89.3 jit_solution(171948624718183116)
XLA Ops:
  0.6 86.0 %layer.1 = (bf16[256,256]{1,0:T(8,128)(2,1)}, bf16[2304,256]{1,0:T(8,128)(2,1)}, bf16[2304,256]{1,0:T(8,128)(2,1)}) custom-call(s32[16]{0:T(128)} %length_ref.1, bf16[256,256]{1,0:T(8,128)(2,1)} %hidden_hbm.1, f32[1,2048]{1,0:T(1,128)} %bitcast.5, f32[1,2048]{1,0:T(1,128)} %bitcast.6, bf16[3,32,256]{2,1,0:T(8,128)(2,1)} %weight_hbm.1, f32[3,256]{1,0:T(4,128)} %bias_hbm.1, ...), custom_call_target="tpu_custom_call" | custom-call | tf_op jit(solution)/shard_map/layer/pallas_call | solution.py:643
  86.6 2.6 %hand_over.1 = (bf16[256,256]{1,0:T(8,128)(2,1)}, bf16[2304,256]{1,0:T(8,128)(2,1)}, bf16[2304,256]{1,0:T(8,128)(2,1)}) custom-call(bf16[256,256]{1,0:T(8,128)(2,1)} %get-tuple-element.6.mixed, bf16[2304,256]{1,0:T(8,128)(2,1)} %get-tuple-element.7.keys, bf16[2304,256]{1,0:T(8,128)(2,1)} %get-tuple-element.8.values), custom_call_target="tpu_custom_call" | custom-call | tf_op jit(solution)/shard_map/hand_over/pallas_call | solution.py:673
